TPU v7x, 256 devices: a whole 4x4x8 slice. The times are simulated.
256 devices in a mesh: trow: 16 (over x, y_lo, core), tcol: 16 (over y_hi, z).
Axes of the slice: x: 4, y: 4 (y_hi: 2, y_lo: 2; y = y_hi * 2 + y_lo), z: 8, core: 2. Of those that a mesh axis runs over, the one named last changes fastest.
Arguments:
- green_lesser: bfloat16 [2, 128, 128, 512], P(None, 'trow', 'tcol'), may hold values from -6 to 6
- green_greater: bfloat16 [2, 128, 128, 512], P(None, 'trow', 'tcol'), may hold values from -6 to 6
- lattice_map: int32 [512], replicated, may hold values from 0 to 511, each once
- time_offset: int32 [1], replicated, may hold values from 0 to 63
Outputs:
- collision_lesser: bfloat16 [2, 128, 128, 512], P(None, 'trow', 'tcol')
- collision_greater: bfloat16 [2, 128, 128, 512], P(None, 'trow', 'tcol')
Inputs may be any that keep to these rules, and one draw needn't show every extreme that they name: `lattice_map`: every lattice momentum index 0 to 511 appears exactly once.
All inputs are finite; a program needn't handle non-finite values.
Results may differ from a plain program's by a relative error of at most 0.011.
Values may be sent and summed in bfloat16 or wider, within the bound.
A program may use at most 64 MiB of HBM per device.

v0:
```python
import math

import jax
import jax.numpy as jnp
import numpy as np
from jax import lax
from jax.experimental import pallas as pl
from jax.experimental.pallas import tpu as pltpu
from jax.sharding import PartitionSpec as P

PERIOD = 64
STEP_SIZE = 0.01
DRIVE_DEPTH = 0.5
MESH = pl.DeviceIdType.MESH
F32 = jnp.float32
BF16 = jnp.bfloat16

N = 16
TILE = 8
K = 512
LANES = N * TILE
CELLS = TILE * TILE
NORM = 1.0 / math.sqrt(K)

NT = (((1,), (1,)), ((), ()))
NN = (((1,), (0,)), ((), ()))


def mm(left, right, dims=NN):
    return lax.dot_general(left, right, dims, preferred_element_type=F32)


def block_swap(parts):
    parts = list(parts)
    lane = lax.broadcasted_iota(jnp.int32, parts[0].shape, 1)
    bit = 1
    while bit < N:
        shift = bit * TILE
        low = (lane // shift) % 2 == 0
        for i in range(N):
            if i & bit:
                continue
            first, second = parts[i], parts[i | bit]
            parts[i] = jnp.where(low, first, pltpu.roll(second, shift, 1))
            parts[i | bit] = jnp.where(low, pltpu.roll(first, LANES - shift, 1), second)
        bit *= 2
    return parts


def kernel(
    map_ref, coupling_ref, lesser_hbm, greater_hbm, table_hbm, out_lesser, out_greater,
    green, table, perm, site, mirror_out, mirror_in, terms, spread,
    ga_out, ga_in, gb_out, gb_in, sa_out, sa_in, sb_out, sb_in, cb_out, cb_in, ca_out, ca_in,
    load_sems, pair_sems, send_sems, recv_sems,
):
    row = lax.axis_index("trow")
    col = lax.axis_index("tcol")
    apart = row != col
    barrier = pltpu.get_barrier_semaphore()

    def greet(step, carry):
        pl.semaphore_signal(
            barrier, inc=1, device_id=(lax.rem(row + step, N), col), device_id_type=MESH
        )
        pl.semaphore_signal(
            barrier, inc=1, device_id=(row, lax.rem(col + step, N)), device_id_type=MESH
        )
        return carry

    @pl.when(apart)
    def _():
        pl.semaphore_signal(barrier, inc=1, device_id=(col, row), device_id_type=MESH)

    lax.fori_loop(1, N, greet, 0)

    load_lesser = pltpu.make_async_copy(lesser_hbm, green.at[0], load_sems.at[0])
    load_greater = pltpu.make_async_copy(greater_hbm, green.at[1], load_sems.at[1])
    load_table = pltpu.make_async_copy(table_hbm, table, load_sems.at[2])
    load_lesser.start()
    load_greater.start()
    load_table.start()

    def along_rows(source, target, phase):
        def one(step, carry):
            other = lax.rem(row + step, N)
            pltpu.make_async_remote_copy(
                src_ref=source.at[other], dst_ref=target.at[row],
                send_sem=send_sems.at[phase, other], recv_sem=recv_sems.at[phase, row],
                device_id=(other, col), device_id_type=MESH,
            ).start()
            return carry

        lax.fori_loop(1, N, one, 0)
        target[pl.ds(row, 1)] = source[pl.ds(row, 1)]

    def rows_arrived(source, target, phase):
        def one(step, carry):
            other = lax.rem(row + N - step, N)
            pltpu.make_async_remote_copy(
                src_ref=source.at[other], dst_ref=target.at[other],
                send_sem=send_sems.at[phase, other], recv_sem=recv_sems.at[phase, other],
                device_id=(other, col), device_id_type=MESH,
            ).wait_recv()
            return carry

        lax.fori_loop(1, N, one, 0)

    def rows_left(source, target, phase):
        def one(step, carry):
            other = lax.rem(row + step, N)
            pltpu.make_async_remote_copy(
                src_ref=source.at[other], dst_ref=target.at[row],
                send_sem=send_sems.at[phase, other], recv_sem=recv_sems.at[phase, row],
                device_id=(other, col), device_id_type=MESH,
            ).wait_send()
            return carry

        lax.fori_loop(1, N, one, 0)

    def col_copy(source, target, phase, other, mine, scatter):
        src = source.at[other] if scatter else source.at[:, :, other]
        dst = target.at[:, :, mine] if scatter else target.at[mine]
        return pltpu.make_async_remote_copy(
            src_ref=src, dst_ref=dst,
            send_sem=send_sems.at[phase, other], recv_sem=recv_sems.at[phase, mine],
            device_id=(row, other), device_id_type=MESH,
        )

    def along_cols(source, target, phase, scatter):
        def one(step, carry):
            col_copy(source, target, phase, lax.rem(col + step, N), col, scatter).start()
            return carry

        lax.fori_loop(1, N, one, 0)
        if scatter:
            target[:, :, pl.ds(col, 1)] = source[pl.ds(col, 1)].reshape(2, 4, 1, TILE, LANES)
        else:
            target[pl.ds(col, 1)] = source[:, :, pl.ds(col, 1)].reshape(1, 2, 4, TILE, LANES)

    def cols_arrived(source, target, phase, scatter):
        def one(step, carry):
            other = lax.rem(col + N - step, N)
            src = source.at[other] if scatter else source.at[:, :, other]
            dst = target.at[:, :, other] if scatter else target.at[other]
            pltpu.make_async_remote_copy(
                src_ref=src, dst_ref=dst,
                send_sem=send_sems.at[phase, other], recv_sem=recv_sems.at[phase, other],
                device_id=(row, other), device_id_type=MESH,
            ).wait_recv()
            return carry

        lax.fori_loop(1, N, one, 0)

    def cols_left(source, target, phase, scatter):
        def one(step, carry):
            col_copy(source, target, phase, lax.rem(col + step, N), col, scatter).wait_send()
            return carry

        lax.fori_loop(1, N, one, 0)

    def rows_to_cols(arrived, outgoing):
        for half in range(2):
            for part in range(2):
                base = part * 16
                swapped = block_swap(
                    [arrived[a, half, base : base + 16, :].astype(F32) for a in range(N)]
                )
                for q in range(N):
                    start = (half * N + q) * 32 + base
                    spread[start : start + 16, :] = swapped[q]
        for m in range(32):
            picked = spread[pl.ds(m, 32, stride=32), :]
            outgoing[m // 2, m % 2] = picked.reshape(4, TILE, LANES).astype(BF16)

    def cols_to_rows(arrived, outgoing):
        for m in range(32):
            spread[m * 32 : (m + 1) * 32, :] = (
                arrived[m // 2, m % 2].astype(F32).reshape(32, LANES)
            )
        for half in range(2):
            for part in range(2):
                base = part * 16
                swapped = block_swap(
                    [
                        spread[pl.ds(base * 32 + half * N + q, 16, stride=32), :]
                        for q in range(N)
                    ]
                )
                for a in range(N):
                    outgoing[a, half, base : base + 16, :] = swapped[a].astype(BF16)

    lattice = lax.broadcasted_iota(jnp.int32, (K, K), 0)
    perm[...] = jnp.where(lattice == map_ref[...], 1.0, 0.0).astype(BF16)
    r = lax.broadcasted_iota(jnp.int32, (2 * CELLS, 2 * CELLS), 0)
    c = lax.broadcasted_iota(jnp.int32, (2 * CELLS, 2 * CELLS), 1)
    swap = jnp.where(
        (r // CELLS == c // CELLS)
        & ((r // TILE) % TILE == c % TILE)
        & (r % TILE == (c // TILE) % TILE),
        1.0,
        0.0,
    ).astype(BF16)

    load_lesser.wait()
    load_greater.wait()
    load_table.wait()
    for half in range(2):
        natural = green[half].astype(F32).reshape(2 * CELLS, K).astype(BF16)
        turned = mm(swap, natural).astype(BF16)
        by_lattice = mm(turned, perm[...], NT).astype(BF16)
        products = mm(by_lattice, table[...])
        cos_re, sin_re = products[:CELLS, :K], products[:CELLS, K:]
        cos_im, sin_im = products[CELLS:, :K], products[CELLS:, K:]
        site[half, 0] = ((cos_re - sin_im) * NORM).astype(BF16)
        site[half, 1] = ((sin_re + cos_im) * NORM).astype(BF16)
        mirror = jnp.concatenate(
            [((cos_re + sin_im) * NORM), ((cos_im - sin_re) * NORM)], axis=0
        ).astype(BF16)
        mirror_out[half] = mm(swap, mirror).astype(BF16)
        spectral = mm(perm[...], turned, NT)
        ga_out[:, half] = spectral.reshape(N, 32, LANES).astype(BF16)

    pl.semaphore_wait(barrier, 2 * (N - 1) + jnp.where(apart, 1, 0))

    @pl.when(apart)
    def _():
        pltpu.make_async_remote_copy(
            src_ref=mirror_out, dst_ref=mirror_in,
            send_sem=pair_sems.at[0], recv_sem=pair_sems.at[1],
            device_id=(col, row), device_id_type=MESH,
        ).start()

    @pl.when(jnp.logical_not(apart))
    def _():
        mirror_in[...] = mirror_out[...]

    along_rows(ga_out, ga_in, 0)

    @pl.when(apart)
    def _():
        pltpu.make_async_remote_copy(
            src_ref=mirror_out, dst_ref=mirror_in,
            send_sem=pair_sems.at[0], recv_sem=pair_sems.at[1],
            device_id=(col, row), device_id_type=MESH,
        ).wait()

    coupling = jnp.concatenate([coupling_ref[...]] * (K // LANES), axis=1)
    for half in range(2):
        first_re, first_im = site[half, 0].astype(F32), site[half, 1].astype(F32)
        other_re = mirror_in[1 - half, :CELLS, :].astype(F32)
        other_im = mirror_in[1 - half, CELLS:, :].astype(F32)
        square_re = first_re * first_re - first_im * first_im
        square_im = 2.0 * first_re * first_im
        self_re = (coupling * (square_re * other_re - square_im * other_im)).astype(BF16)
        self_im = (coupling * (square_re * other_im + square_im * other_re)).astype(BF16)
        terms[:CELLS, :K] = self_re
        terms[:CELLS, K:] = self_im
        terms[CELLS:, :K] = self_im
        terms[CELLS:, K:] = -self_re
        spectral = mm(table[...], terms[...], NT) * NORM
        sa_out[:, half] = spectral.reshape(N, 32, LANES).astype(BF16)
    along_rows(sa_out, sa_in, 1)

    rows_arrived(ga_out, ga_in, 0)
    rows_to_cols(ga_in, gb_out)
    along_cols(gb_out, gb_in, 2, True)
    rows_arrived(sa_out, sa_in, 1)
    rows_to_cols(sa_in, sb_out)
    along_cols(sb_out, sb_in, 3, True)
    cols_arrived(gb_out, gb_in, 2, True)
    cols_arrived(sb_out, sb_in, 3, True)

    down = lax.broadcasted_iota(jnp.int32, (LANES, LANES), 0)
    across = lax.broadcasted_iota(jnp.int32, (LANES, LANES), 1)
    for k in range(2):
        g = [gb_in[k, i].astype(F32).reshape(LANES, LANES) for i in range(4)]
        s = [sb_in[k, i].astype(F32).reshape(LANES, LANES) for i in range(4)]
        retarded = [jnp.where(down <= across, s[2 + i] - s[i], 0.0).astype(BF16) for i in range(2)]
        advanced = [jnp.where(across <= down, g[i] - g[2 + i], 0.0) for i in range(2)]
        for half in range(2):
            g_re, g_im = g[2 * half], g[2 * half + 1]
            left = jnp.concatenate(
                [
                    jnp.concatenate([g_re, -g_im, advanced[0], -advanced[1]], axis=1),
                    jnp.concatenate([g_im, g_re, advanced[1], advanced[0]], axis=1),
                ],
                axis=0,
            ).astype(BF16)
            right = jnp.concatenate(
                retarded + [s[2 * half].astype(BF16), s[2 * half + 1].astype(BF16)], axis=0
            )
            total = (mm(left, right) * STEP_SIZE).reshape(2, N, TILE, LANES).astype(BF16)
            cb_out[k, 2 * half] = total[0]
            cb_out[k, 2 * half + 1] = total[1]
    along_cols(cb_out, cb_in, 4, False)
    cols_arrived(cb_out, cb_in, 4, False)
    cols_to_rows(cb_in, ca_out)
    along_rows(ca_out, ca_in, 5)
    rows_arrived(ca_out, ca_in, 5)
    for half, out in enumerate((out_lesser, out_greater)):
        full = ca_in[:, half].reshape(K, LANES)
        cells = mm(swap, full, NT).astype(BF16)
        out[...] = mm(cells, perm[...]).reshape(2, TILE, TILE, K).astype(BF16)

    rows_left(ga_out, ga_in, 0)
    rows_left(sa_out, sa_in, 1)
    cols_left(gb_out, gb_in, 2, True)
    cols_left(sb_out, sb_in, 3, True)
    cols_left(cb_out, cb_in, 4, False)
    rows_left(ca_out, ca_in, 5)


def tables():
    index = np.arange(K, dtype=np.int64)
    phases = (index[:, None] * index[None, :] % K).astype(np.float32) * np.float32(
        2.0 * math.pi / K
    )
    return np.concatenate([np.cos(phases), np.sin(phases)], axis=1).astype(jnp.bfloat16)


def body(green_lesser, green_greater, lattice_map, time_offset):
    steps = jnp.arange(TILE, dtype=jnp.int32)

    def line(block):
        at = (time_offset[0] + block * TILE + steps) % PERIOD
        return 1.0 + DRIVE_DEPTH * jnp.cos(at.astype(F32) * (2.0 * math.pi / PERIOD))

    pairs = line(lax.axis_index("tcol"))[:, None] * line(lax.axis_index("trow"))[None, :]
    coupling = jnp.broadcast_to(pairs[:, :, None], (TILE, TILE, LANES)).reshape(CELLS, LANES)
    any_spec = pl.BlockSpec(memory_space=pl.ANY)
    vmem_spec = pl.BlockSpec(memory_space=pltpu.VMEM)
    tile = jax.ShapeDtypeStruct((2, TILE, TILE, K), BF16)
    by_row = pltpu.VMEM((N, 2, 32, LANES), BF16)
    by_col = pltpu.VMEM((N, 2, 4, TILE, LANES), BF16)
    window = pltpu.VMEM((2, 4, N, TILE, LANES), BF16)
    return pl.pallas_call(
        kernel,
        out_shape=(tile, tile),
        in_specs=[vmem_spec, vmem_spec, any_spec, any_spec, any_spec],
        out_specs=(vmem_spec, vmem_spec),
        scratch_shapes=[
            pltpu.VMEM((2, 2, TILE, TILE, K), BF16),
            pltpu.VMEM((K, 2 * K), BF16),
            pltpu.VMEM((K, K), BF16),
            pltpu.VMEM((2, 2, CELLS, K), BF16),
            pltpu.VMEM((2, 2 * CELLS, K), BF16),
            pltpu.VMEM((2, 2 * CELLS, K), BF16),
            pltpu.VMEM((2 * CELLS, 2 * K), BF16),
            pltpu.VMEM((1024, LANES), F32),
            by_row, by_row, by_col, window,
            by_row, by_row, by_col, window,
            window, by_col, by_row, by_row,
            pltpu.SemaphoreType.DMA((3,)),
            pltpu.SemaphoreType.DMA((2,)),
            pltpu.SemaphoreType.DMA((6, N)),
            pltpu.SemaphoreType.DMA((6, N)),
        ],
        compiler_params=pltpu.CompilerParams(
            collective_id=0, has_side_effects=True, vmem_limit_bytes=48 * 1024 * 1024
        ),
    )(lattice_map.reshape(1, K), coupling, green_lesser, green_greater, jnp.asarray(tables()))


def solution(mesh):
    in_specs = (P(None, "trow", "tcol", None), P(None, "trow", "tcol", None), P(), P())
    out_specs = (P(None, "trow", "tcol", None), P(None, "trow", "tcol", None))
    return jax.shard_map(body, mesh=mesh, in_specs=in_specs, out_specs=out_specs, check_vma=False)
```

profile of v0, /device:TPU:1, one launch (start us, length us, event | category | flops | bytes accessed | tf_op | source)
XLA Modules:
  0.0 74.4 jit_solution(12381443891301454732)
XLA Ops:
  1.3 0.1 fusion.4
  1.3 0.1 fusion.9
  1.4 0.1 mul.64
  1.5 0.1 mul.58
  1.6 0.1 mul.59
  1.6 0.0 copy-start.3
  1.7 0.1 broadcast_in_dim.2.coupling_ref
  1.7 0.6 copy-done.3
  2.3 0.0 copy-start
  2.3 1.2 %copy-done = bf16[512,1024]{1,0:T(8,128)(2,1)S(1)} copy-done((bf16[512,1024]{1,0:T(8,128)(2,1)S(1)}, bf16[512,1024]{1,0:T(8,128)(2,1)}, u32[]{:S(2)}) %copy-start) | copy-done | bytes 1048600
  3.6 0.0 copy-start.1
  3.6 0.9 %copy-done.1 = bf16[2,8,8,512]{3,2,1,0:T(8,128)(2,1)S(1)} copy-done((bf16[2,8,8,512]{3,2,1,0:T(8,128)(2,1)S(1)}, bf16[2,8,8,512]{3,2,1,0:T(8,128)(2,1)}, u32[]{:S(2)}) %copy-start.1) | copy-done | bytes 131096
  4.5 0.0 copy-start.2
  4.5 0.9 %copy-done.2 = bf16[2,8,8,512]{3,2,1,0:T(8,128)(2,1)S(1)} copy-done((bf16[2,8,8,512]{3,2,1,0:T(8,128)(2,1)S(1)}, bf16[2,8,8,512]{3,2,1,0:T(8,128)(2,1)}, u32[]{:S(2)}) %copy-start.2) | copy-done | bytes 131096
  5.4 67.7 %shard_map.68 = (bf16[2,8,8,512]{3,2,1,0:T(8,128)(2,1)S(1)}, bf16[2,8,8,512]{3,2,1,0:T(8,128)(2,1)S(1)}) custom-call(s32[1,512]{1,0:T(1,128)S(1)} %bitcast.6, f32[64,128]{1,0:T(8,128)S(1)} %broadcast_in_dim.2.coupling_ref, bf16[2,8,8,512]{3,2,1,0:T(8,128)(2,1)S(1)} %copy-done.1, bf16[2,8,8,512]{3,2,1,0:T(8,128)(2,1)S(1)} %copy-done.2, ...), custom_call_target="tpu_custom_call" | custom-call | tf_op jit(solution)/shard_map/pallas_call | solution.py:336
  73.1 0.7 copy.10
  73.7 0.7 copy.11
  (2 shorter events, 0.0 us)
Async XLA Ops:
  1.6 0.7 copy-start.3
  2.3 1.2 %copy-start = (bf16[512,1024]{1,0:T(8,128)(2,1)S(1)}, bf16[512,1024]{1,0:T(8,128)(2,1)}, u32[]{:S(2)}) copy-start(bf16[512,1024]{1,0:T(8,128)(2,1)} %constant.37.clone.table_hbm) | copy-start | bytes 3145732
  3.6 0.9 %copy-start.1 = (bf16[2,8,8,512]{3,2,1,0:T(8,128)(2,1)S(1)}, bf16[2,8,8,512]{3,2,1,0:T(8,128)(2,1)}, u32[]{:S(2)}) copy-start(bf16[2,8,8,512]{3,2,1,0:T(8,128)(2,1)} %lesser_hbm.1) | copy-start | bytes 393220
  4.5 0.9 %copy-start.2 = (bf16[2,8,8,512]{3,2,1,0:T(8,128)(2,1)S(1)}, bf16[2,8,8,512]{3,2,1,0:T(8,128)(2,1)}, u32[]{:S(2)}) copy-start(bf16[2,8,8,512]{3,2,1,0:T(8,128)(2,1)} %greater_hbm.1) | copy-start | bytes 393220
where the time goes:
time: 74.6 us; the launch traced here: 74.4 us
  Pallas kernels  67.7 us (91%)
  local copies, waits for them, and re-layouts  5.26 us (7%)
  between operations  1.32 us (2%)
    pallas_call x1, Pallas kernels, body(): pl.pallas_call(kernel, out_shape=(tile, tile), in_specs=[vmem_spec, vmem_...  67.7 us
    unnamed x10, local copies, waits for them, and re-layouts  4.95 us

commit v1 on v0

v1 whole, which is shorter than its diff:
```python
import math

import jax
import jax.numpy as jnp
import numpy as np
from jax import lax
from jax.experimental import pallas as pl
from jax.experimental.pallas import tpu as pltpu
from jax.sharding import PartitionSpec as P

PERIOD = 64
STEP_SIZE = 0.01
DRIVE_DEPTH = 0.5
MESH = pl.DeviceIdType.MESH
F32 = jnp.float32
BF16 = jnp.bfloat16

N = 16
TILE = 8
K = 512
BLOCK = K // N
LANES = N * TILE
WIDE = TILE * LANES
CELLS = TILE * TILE
NORM = 1.0 / math.sqrt(K)

NT = (((1,), (1,)), ((), ()))
NN = (((1,), (0,)), ((), ()))

SITE, MIRROR, INNER, SIGMA, GREEN_A, GREEN_B, OUT_B, OUT_A = range(8)


def mm(left, right, dims=NN):
    return lax.dot_general(left, right, dims, preferred_element_type=F32)


def block_swap(parts):
    parts = list(parts)
    lane = lax.broadcasted_iota(jnp.int32, parts[0].shape, 1)
    bit = 1
    while bit < N:
        shift = bit * TILE
        low = (lane // shift) % 2 == 0
        for i in range(N):
            if i & bit:
                continue
            first, second = parts[i], parts[i | bit]
            parts[i] = jnp.where(low, first, pltpu.roll(second, shift, 1))
            parts[i | bit] = jnp.where(low, pltpu.roll(first, LANES - shift, 1), second)
        bit *= 2
    return parts


def one_hot(hit):
    return jnp.where(hit, 1.0, 0.0).astype(BF16)


def kernel(
    offset_ref, map_hbm, lesser_hbm, greater_hbm, table_hbm, inner_hbm, outer_hbm,
    out_lesser, out_greater,
    momentum_map, green, table, inner, outer, perm, spread, own, mirror, selves,
    site_out, site_in, mirror_in, y_out, y_in, s_out, s_in,
    ga_out, ga_in, gb_out, gb_in, lefts, cb_out, cb_in, ca_out, ca_in,
    load_sems, send_sems, recv_sems,
):
    row = lax.axis_index("trow")
    col = lax.axis_index("tcol")
    barrier = pltpu.get_barrier_semaphore()

    def greet(step, carry):
        pl.semaphore_signal(
            barrier, inc=1, device_id=(lax.rem(row + step, N), col), device_id_type=MESH
        )
        pl.semaphore_signal(
            barrier, inc=1, device_id=(row, lax.rem(col + step, N)), device_id_type=MESH
        )
        return carry

    loads = [
        pltpu.make_async_copy(source, target, load_sems.at[i])
        for i, (source, target) in enumerate(
            (
                (map_hbm, momentum_map),
                (lesser_hbm, green.at[0]),
                (greater_hbm, green.at[1]),
                (table_hbm, table),
                (inner_hbm.at[row], inner),
                (outer_hbm, outer),
            )
        )
    ]
    for load in loads:
        load.start()
    lax.fori_loop(1, N, greet, 0)

    def row_copy(source, target, phase, other, slot):
        return pltpu.make_async_remote_copy(
            src_ref=source.at[other], dst_ref=target.at[slot],
            send_sem=send_sems.at[phase, other], recv_sem=recv_sems.at[phase, slot],
            device_id=(other, col), device_id_type=MESH,
        )

    def along_rows(source, target, phase):
        def one(step, carry):
            row_copy(source, target, phase, lax.rem(row + step, N), row).start()
            return carry

        lax.fori_loop(1, N, one, 0)
        target[pl.ds(row, 1)] = source[pl.ds(row, 1)]

    def rows_arrived(source, target, phase):
        def one(step, carry):
            other = lax.rem(row + N - step, N)
            row_copy(source, target, phase, other, other).wait_recv()
            return carry

        lax.fori_loop(1, N, one, 0)

    def rows_left(source, target, phase):
        def one(step, carry):
            row_copy(source, target, phase, lax.rem(row + step, N), row).wait_send()
            return carry

        lax.fori_loop(1, N, one, 0)

    plain = (lambda ref, i: ref.at[i], lambda ref, i: ref.at[i])
    to_window = (lambda ref, i: ref.at[i], lambda ref, i: ref.at[:, :, i])
    from_window = (lambda ref, i: ref.at[:, :, i], lambda ref, i: ref.at[i])

    def col_copy(source, target, phase, other, slot, form):
        return pltpu.make_async_remote_copy(
            src_ref=form[0](source, other), dst_ref=form[1](target, slot),
            send_sem=send_sems.at[phase, other], recv_sem=recv_sems.at[phase, slot],
            device_id=(row, other), device_id_type=MESH,
        )

    def along_cols(source, target, phase, form):
        def one(step, carry):
            col_copy(source, target, phase, lax.rem(col + step, N), col, form).start()
            return carry

        lax.fori_loop(1, N, one, 0)

    def cols_arrived(source, target, phase, form):
        def one(step, carry):
            other = lax.rem(col + N - step, N)
            col_copy(source, target, phase, other, other, form).wait_recv()
            return carry

        lax.fori_loop(1, N, one, 0)

    def cols_left(source, target, phase, form):
        def one(step, carry):
            col_copy(source, target, phase, lax.rem(col + step, N), col, form).wait_send()
            return carry

        lax.fori_loop(1, N, one, 0)

    place = lax.broadcasted_iota(jnp.int32, (K, 1), 0)
    loads[0].wait()
    perm[...] = one_hot((place // BLOCK) + N * (place % BLOCK) == momentum_map[...])
    r = lax.broadcasted_iota(jnp.int32, (LANES, LANES), 0)
    c = lax.broadcasted_iota(jnp.int32, (LANES, LANES), 1)
    swap = one_hot(
        (r // CELLS == c // CELLS)
        & ((r // TILE) % TILE == c % TILE)
        & (r % TILE == (c // TILE) % TILE)
    )

    for load in loads[1:]:
        load.wait()
    turned = []
    for half in range(2):
        natural = green[half].astype(F32).reshape(2 * CELLS, K).astype(BF16)
        turned.append(mm(swap, natural).astype(BF16))
        ordered = mm(turned[half], perm[...], NT)
        g_re, g_im = ordered[:CELLS], ordered[CELLS:]
        pairs = jnp.concatenate(
            [jnp.concatenate([g_re, -g_im], axis=1), jnp.concatenate([g_im, g_re], axis=1)],
            axis=0,
        ).astype(BF16)
        sites = mm(table[...], pairs, NT) * NORM
        site_out[:, half] = sites.reshape(N, BLOCK, LANES).astype(BF16)

    pl.semaphore_wait(barrier, 2 * (N - 1))
    along_rows(site_out, site_in, SITE)
    for half in range(2):
        spectral = mm(perm[...], turned[half], NT)
        ga_out[:, half] = spectral.reshape(N, BLOCK, LANES).astype(BF16)
    along_rows(ga_out, ga_in, GREEN_A)

    def pass_on(other):
        @pl.when(other != col)
        def _():
            col_copy(site_in, mirror_in, MIRROR, other, col, plain).start()

        @pl.when(other == col)
        def _():
            mirror_in[pl.ds(col, 1)] = site_in[pl.ds(col, 1)]

    pass_on(row)

    def relay(step, carry):
        other = lax.rem(row + N - step, N)
        row_copy(site_out, site_in, SITE, other, other).wait_recv()
        pass_on(other)
        return carry

    lax.fori_loop(1, N, relay, 0)

    for half in range(2):
        for part in range(2):
            base = part * 16
            swapped = block_swap(
                [site_in[a, half, base : base + 16, :].astype(F32) for a in range(N)]
            )
            for q in range(N):
                at, lane = (q // TILE) * BLOCK + base, (q % TILE) * LANES
                own[half, at : at + 16, lane : lane + LANES] = swapped[q].astype(BF16)

    rows_arrived(ga_out, ga_in, GREEN_A)
    for half in range(2):
        for part in range(2):
            base = part * 16
            swapped = block_swap(
                [ga_in[a, half, base : base + 16, :].astype(F32) for a in range(N)]
            )
            for q in range(N):
                start = (half * N + q) * BLOCK + base
                spread[start : start + 16, :] = swapped[q]
    for m in range(BLOCK):
        picked = spread[pl.ds(m, BLOCK, stride=BLOCK), :]
        gb_out[m // 2, m % 2] = picked.reshape(4, TILE, LANES).astype(BF16)
    along_cols(gb_out, gb_in, GREEN_B, to_window)
    gb_in[:, :, pl.ds(col, 1)] = gb_out[pl.ds(col, 1)].reshape(2, 4, 1, TILE, LANES)

    steps = lax.broadcasted_iota(jnp.int32, (TILE, LANES), 1)
    late = lax.broadcasted_iota(jnp.int32, (TILE, LANES), 0) + col * TILE

    def drive(at):
        phase = ((offset_ref[0] + at) % PERIOD).astype(F32) * (2.0 * math.pi / PERIOD)
        return 1.0 + DRIVE_DEPTH * jnp.cos(phase)

    product = drive(late) * drive(steps)
    coupling = jnp.concatenate([product[i : i + 1] for i in range(TILE)], axis=1)
    fr = lax.broadcasted_iota(jnp.int32, (2 * BLOCK, 2 * BLOCK), 0)
    fc = lax.broadcasted_iota(jnp.int32, (2 * BLOCK, 2 * BLOCK), 1)
    first_run = (fc // 16) % 2 == 0
    inside = fc + jnp.where(first_run, 16, -16)
    edge = (fc // 16) * 16 + jnp.where(first_run, (16 - fc % 16) % 16, 15 - fc % 16)
    flip = one_hot(fr == inside + jnp.where(row == 0, 1, 0) * (edge - inside))

    cols_arrived(site_in, mirror_in, MIRROR, plain)
    spread[...] = mm(mirror_in[...].reshape(2 * K, LANES), swap)
    for half in range(2):
        for part in range(2):
            base = part * 16
            swapped = block_swap(
                [
                    spread[pl.ds(b * 2 * BLOCK + half * BLOCK + base, 16), :]
                    for b in range(N)
                ]
            )
            for q in range(N):
                at, lane = (q // TILE) * BLOCK + base, (q % TILE) * LANES
                mirror[half, at : at + 16, lane : lane + LANES] = swapped[q].astype(BF16)
    for half in range(2):
        first_re, first_im = own[half, :BLOCK].astype(F32), own[half, BLOCK:].astype(F32)
        other = mm(flip, mirror[1 - half])
        other_re, other_im = other[:BLOCK], other[BLOCK:]
        square_re = first_re * first_re - first_im * first_im
        square_im = 2.0 * first_re * first_im
        self_re = coupling * (square_re * other_re - square_im * other_im)
        self_im = coupling * (square_re * other_im + square_im * other_re)
        at = half * 2 * BLOCK
        selves[at : at + BLOCK] = self_re.astype(BF16)
        selves[at + BLOCK : at + 2 * BLOCK] = self_im.astype(BF16)
    doubled = jnp.concatenate([selves[...], selves[...]], axis=0)
    y_out[...] = mm(inner[...], doubled).reshape(N, TILE, WIDE).astype(BF16)
    along_rows(y_out, y_in, INNER)

    down = lax.broadcasted_iota(jnp.int32, (LANES, LANES), 0)
    across = lax.broadcasted_iota(jnp.int32, (LANES, LANES), 1)
    cols_arrived(gb_out, gb_in, GREEN_B, to_window)
    for k in range(2):
        g = [gb_in[k, i].astype(F32).reshape(LANES, LANES) for i in range(4)]
        advanced = [jnp.where(across <= down, g[i] - g[2 + i], 0.0) for i in range(2)]
        for half in range(2):
            g_re, g_im = g[2 * half], g[2 * half + 1]
            for i, blocks in enumerate(
                ([g_re, -g_im, advanced[0], -advanced[1]], [g_im, g_re, advanced[1], advanced[0]])
            ):
                lefts[k, half, i * LANES : (i + 1) * LANES, :] = jnp.concatenate(
                    blocks, axis=1
                ).astype(BF16)

    rows_arrived(y_out, y_in, INNER)
    arrived = y_in[...].astype(F32).reshape(LANES, WIDE).astype(BF16)
    sigma = mm(outer[...], jnp.concatenate([arrived, arrived], axis=0)) * NORM
    s_out[...] = sigma.reshape(N, TILE, WIDE).astype(BF16)
    along_cols(s_out, s_in, SIGMA, plain)
    s_in[pl.ds(col, 1)] = s_out[pl.ds(col, 1)]
    cols_arrived(s_out, s_in, SIGMA, plain)
    for b in range(N):
        for t in range(TILE):
            start = (b * TILE + t) * TILE
            spread[start : start + TILE, :] = s_in[b, :, t * LANES : (t + 1) * LANES].astype(F32)
    for k in range(2):
        s = [spread[pl.ds(4 * k + i, LANES, stride=TILE), :] for i in range(4)]
        retarded = [jnp.where(down <= across, s[2 + i] - s[i], 0.0) for i in range(2)]
        for half in range(2):
            right = jnp.concatenate(
                retarded + [s[2 * half], s[2 * half + 1]], axis=0
            ).astype(BF16)
            total = mm(lefts[k, half], right) * STEP_SIZE
            total = total.reshape(2, N, TILE, LANES).astype(BF16)
            cb_out[k, 2 * half] = total[0]
            cb_out[k, 2 * half + 1] = total[1]
    along_cols(cb_out, cb_in, OUT_B, from_window)
    cb_in[pl.ds(col, 1)] = cb_out[:, :, pl.ds(col, 1)].reshape(1, 2, 4, TILE, LANES)
    cols_arrived(cb_out, cb_in, OUT_B, from_window)
    for m in range(BLOCK):
        spread[m * BLOCK : (m + 1) * BLOCK, :] = (
            cb_in[m // 2, m % 2].astype(F32).reshape(BLOCK, LANES)
        )
    for half in range(2):
        for part in range(2):
            base = part * 16
            swapped = block_swap(
                [
                    spread[pl.ds(base * BLOCK + half * N + q, 16, stride=BLOCK), :]
                    for q in range(N)
                ]
            )
            for a in range(N):
                ca_out[a, half, base : base + 16, :] = swapped[a].astype(BF16)
    along_rows(ca_out, ca_in, OUT_A)
    rows_arrived(ca_out, ca_in, OUT_A)
    for half, out in enumerate((out_lesser, out_greater)):
        full = ca_in[:, half].reshape(K, LANES)
        cells = mm(swap, full, NT).astype(BF16)
        out[...] = mm(cells, perm[...]).reshape(2, TILE, TILE, K).astype(BF16)

    def passed_on(step, carry):
        other = lax.rem(row + step, N)

        @pl.when(other != col)
        def _():
            col_copy(site_in, mirror_in, MIRROR, other, col, plain).wait_send()

        return carry

    lax.fori_loop(0, N, passed_on, 0)
    rows_left(site_out, site_in, SITE)
    rows_left(ga_out, ga_in, GREEN_A)
    cols_left(gb_out, gb_in, GREEN_B, to_window)
    rows_left(y_out, y_in, INNER)
    cols_left(s_out, s_in, SIGMA, plain)
    cols_left(cb_out, cb_in, OUT_B, from_window)
    rows_left(ca_out, ca_in, OUT_A)


def sites_of(block):
    run = 32 * np.arange(16)
    if block == 0:
        return np.concatenate([run, 16 + run])
    return np.concatenate([block + run, (-block - run) % K])


def split(matrix):
    high = matrix.astype(jnp.bfloat16)
    low = (matrix - high.astype(np.float64)).astype(jnp.bfloat16)
    return np.concatenate([high, low], axis=-1)


def inverse_block(angle):
    cos, sin = np.cos(angle), np.sin(angle)
    return np.stack([np.stack([cos, sin], -1), np.stack([-sin, cos], -1)], -2)


def constants():
    order = (np.arange(K) // BLOCK) + N * (np.arange(K) % BLOCK)
    sites = np.concatenate([sites_of(block) for block in range(N)])
    phases = (sites[:, None] * order[None, :] % K).astype(np.float32) * np.float32(
        2.0 * math.pi / K
    )
    table = np.concatenate([np.cos(phases), np.sin(phases)], axis=1).astype(jnp.bfloat16)
    inner = np.zeros((N, N, 2, 2, 2, 2, 2, 2, 16))
    for block in range(N):
        near = sites_of(block).reshape(2, 16)
        angle = 2.0 * math.pi / K * (np.arange(N)[:, None, None] * near[None] % K)
        turn = inverse_block(angle)
        for half in range(2):
            for run in range(2):
                inner[block, :, half, :, run, half, :, run, :] = turn[:, run].transpose(0, 2, 3, 1)
    residues = np.array([[0, 16]] + [[b, 32 - b] for b in range(1, N)])
    angle = 2.0 * math.pi / 32 * (np.arange(32)[:, None, None] * residues[None] % 32)
    turn = inverse_block(angle)
    outer = np.zeros((32, 2, 2, N, 2, 2, 2))
    for half in range(2):
        outer[:, half, :, :, half] = turn.transpose(0, 3, 1, 4, 2)
    return table, split(inner.reshape(N, LANES, LANES)), split(outer.reshape(LANES, LANES))


def body(green_lesser, green_greater, lattice_map, time_offset):
    hbm = pl.BlockSpec(memory_space=pltpu.MemorySpace.HBM)
    vmem = pl.BlockSpec(memory_space=pltpu.MemorySpace.VMEM)
    tile = jax.ShapeDtypeStruct((2, TILE, TILE, K), BF16)
    by_row = pltpu.VMEM((N, 2, BLOCK, LANES), BF16)
    by_col = pltpu.VMEM((N, 2, 4, TILE, LANES), BF16)
    wide = pltpu.VMEM((N, TILE, WIDE), BF16)
    window = pltpu.VMEM((2, 4, N, TILE, LANES), BF16)
    halves = pltpu.VMEM((2, 2 * BLOCK, WIDE), BF16)
    return pl.pallas_call(
        kernel,
        out_shape=(tile, tile),
        in_specs=[pl.BlockSpec(memory_space=pltpu.MemorySpace.SMEM)] + [hbm] * 6,
        out_specs=(vmem, vmem),
        scratch_shapes=[
            pltpu.VMEM((1, K), jnp.int32),
            pltpu.VMEM((2, 2, TILE, TILE, K), BF16),
            pltpu.VMEM((K, 2 * K), BF16),
            pltpu.VMEM((LANES, 2 * LANES), BF16),
            pltpu.VMEM((LANES, 2 * LANES), BF16),
            pltpu.VMEM((K, K), BF16),
            pltpu.VMEM((2 * K, LANES), F32),
            halves, halves,
            pltpu.VMEM((LANES, WIDE), BF16),
            by_row, by_row, by_row,
            wide, wide, wide, wide,
            by_row, by_row, by_col, window,
            pltpu.VMEM((2, 2, 2 * LANES, 4 * LANES), BF16),
            window, by_col, by_row, by_row,
            pltpu.SemaphoreType.DMA((6,)),
            pltpu.SemaphoreType.DMA((8, N)),
            pltpu.SemaphoreType.DMA((8, N)),
        ],
        compiler_params=pltpu.CompilerParams(
            collective_id=0, has_side_effects=True, vmem_limit_bytes=67_043_328
        ),
    )(
        time_offset, lattice_map.reshape(1, K), green_lesser, green_greater,
        *(jnp.asarray(value) for value in constants()),
    )


def solution(mesh):
    in_specs = (P(None, "trow", "tcol", None), P(None, "trow", "tcol", None), P(), P())
    out_specs = (P(None, "trow", "tcol", None), P(None, "trow", "tcol", None))
    return jax.shard_map(body, mesh=mesh, in_specs=in_specs, out_specs=out_specs, check_vma=False)
```

time: 74.6 us -> 67.2 us (0.901)
  Pallas kernels: 67.7 us -> 63.5 us
  local copies, waits for them, and re-layouts: 5.26 us -> 2.26 us
    pallas_call x1, Pallas kernels: 67.7 us -> 63.5 us  [body(): pl.pallas_call(kernel, out_shape=(tile, tile), in_specs=[pl.BlockSpec(mem...]
    unnamed x10 -> x4, local copies, waits for them, and re-layouts: 4.95 us -> 2.26 us
where the time goes in v1:
time: 67.2 us; the launch traced here: 67.1 us
  Pallas kernels  63.5 us (94%)
  local copies, waits for them, and re-layouts  2.26 us (3%)
  between operations  1.29 us (2%)
    pallas_call x1, Pallas kernels, body(): pl.pallas_call(kernel, out_shape=(tile, tile), in_specs=[pl.BlockSpec(mem...  63.5 us
    unnamed x4, local copies, waits for them, and re-layouts  2.26 us

profile of v1, /device:TPU:1, one launch (start us, length us, event | category | flops | bytes accessed | tf_op | source)
XLA Modules:
  0.0 67.1 jit_solution(3566593693990961096)
XLA Ops:
  1.3 63.5 %shard_map.86 = (bf16[2,8,8,512]{3,2,1,0:T(8,128)(2,1)}, bf16[2,8,8,512]{3,2,1,0:T(8,128)(2,1)}) custom-call(s32[1]{0:T(128)S(6)} %copy.11.offset_ref, s32[1,512]{1,0:T(1,128)} %bitcast.1, bf16[2,8,8,512]{3,2,1,0:T(8,128)(2,1)} %lesser_hbm.1, bf16[2,8,8,512]{3,2,1,0:T(8,128)(2,1)} %greater_hbm.1, bf16[512,1024]{1,0:T(8,128)(2,1)} %constant.6.clone.table_hbm, ...), custom_call_target="tpu_custom_call" | custom-call | tf_op jit(solution)/shard_map/pallas_call | solution.py:414
  64.8 0.0 copy-start
  64.8 1.6 %copy.12 = bf16[2,8,8,512]{3,2,1,0:T(8,128)(2,1)} copy(bf16[2,8,8,512]{3,2,1,0:T(8,128)(2,1)} %get-tuple-element.4) | data formatting | bytes 262144
  66.4 0.0 copy-done
  66.4 0.7 copy.13
Async XLA Ops:
  64.8 1.6 %copy-start = (bf16[2,8,8,512]{3,2,1,0:T(8,128)(2,1)S(1)}, bf16[2,8,8,512]{3,2,1,0:T(8,128)(2,1)}, u32[]{:S(2)}) copy-start(bf16[2,8,8,512]{3,2,1,0:T(8,128)(2,1)} %get-tuple-element.5) | copy-start | bytes 393220

commit v2 on v1

--- a/solution.py
+++ b/solution.py
@@ -27,7 +27,28 @@
 NT = (((1,), (1,)), ((), ()))
 NN = (((1,), (0,)), ((), ()))
 
-SITE, MIRROR, INNER, SIGMA, GREEN_A, GREEN_B, OUT_B, OUT_A = range(8)
+SITE, MIRROR, INNER, SIGMA, GREEN_A, GREEN_B = range(6)
+
+ROW_OFFSETS = sorted(
+    ((x, y, c) for x in (2, 1, -1, 0) for y in (1, 0) for c in (0, 1)),
+    key=lambda o: -(abs(o[0]) + o[1] + 0.2 * o[2]),
+)[:-1]
+COL_OFFSETS = sorted(
+    ((y, z) for z in (4, 3, -3, 2, -2, 1, -1, 0) for y in (1, 0)),
+    key=lambda o: -(abs(o[1]) + 2 * o[0]),
+)
+
+
+def row_at(row, offset, sign=1):
+    x, y, c = row // 4, (row // 2) % 2, row % 2
+    dx, dy, dc = offset
+    return ((x + sign * dx + 4) % 4) * 4 + ((y + dy) % 2) * 2 + (c + dc) % 2
+
+
+def col_at(col, offset, sign=1):
+    y, z = col // 8, col % 8
+    dy, dz = offset
+    return ((y + dy) % 2) * 8 + (z + sign * dz + 8) % 8
 
 
 def mm(left, right, dims=NN):
@@ -60,21 +81,12 @@
     out_lesser, out_greater,
     momentum_map, green, table, inner, outer, perm, spread, own, mirror, selves,
     site_out, site_in, mirror_in, y_out, y_in, s_out, s_in,
-    ga_out, ga_in, gb_out, gb_in, lefts, cb_out, cb_in, ca_out, ca_in,
-    load_sems, send_sems, recv_sems,
+    ga_out, ga_in, gb_out, gb_in, lefts, results, select, x_out, x_in,
+    load_sems, send_sems, recv_sems, tile_sems,
 ):
     row = lax.axis_index("trow")
     col = lax.axis_index("tcol")
     barrier = pltpu.get_barrier_semaphore()
-
-    def greet(step, carry):
-        pl.semaphore_signal(
-            barrier, inc=1, device_id=(lax.rem(row + step, N), col), device_id_type=MESH
-        )
-        pl.semaphore_signal(
-            barrier, inc=1, device_id=(row, lax.rem(col + step, N)), device_id_type=MESH
-        )
-        return carry
 
     loads = [
         pltpu.make_async_copy(source, target, load_sems.at[i])
@@ -91,7 +103,14 @@
     ]
     for load in loads:
         load.start()
-    lax.fori_loop(1, N, greet, 0)
+    for offset in COL_OFFSETS[:-1]:
+        pl.semaphore_signal(
+            barrier, inc=1, device_id=(row, col_at(col, offset)), device_id_type=MESH
+        )
+    for offset in ROW_OFFSETS:
+        pl.semaphore_signal(
+            barrier, inc=1, device_id=(row_at(row, offset), col), device_id_type=MESH
+        )
 
     def row_copy(source, target, phase, other, slot):
         return pltpu.make_async_remote_copy(
@@ -101,31 +120,21 @@
         )
 
     def along_rows(source, target, phase):
-        def one(step, carry):
-            row_copy(source, target, phase, lax.rem(row + step, N), row).start()
-            return carry
-
-        lax.fori_loop(1, N, one, 0)
+        for offset in ROW_OFFSETS:
+            row_copy(source, target, phase, row_at(row, offset), row).start()
         target[pl.ds(row, 1)] = source[pl.ds(row, 1)]
 
     def rows_arrived(source, target, phase):
-        def one(step, carry):
-            other = lax.rem(row + N - step, N)
+        for offset in ROW_OFFSETS:
+            other = row_at(row, offset, -1)
             row_copy(source, target, phase, other, other).wait_recv()
-            return carry
-
-        lax.fori_loop(1, N, one, 0)
 
     def rows_left(source, target, phase):
-        def one(step, carry):
-            row_copy(source, target, phase, lax.rem(row + step, N), row).wait_send()
-            return carry
-
-        lax.fori_loop(1, N, one, 0)
+        for offset in ROW_OFFSETS:
+            row_copy(source, target, phase, row_at(row, offset), row).wait_send()
 
     plain = (lambda ref, i: ref.at[i], lambda ref, i: ref.at[i])
     to_window = (lambda ref, i: ref.at[i], lambda ref, i: ref.at[:, :, i])
-    from_window = (lambda ref, i: ref.at[:, :, i], lambda ref, i: ref.at[i])
 
     def col_copy(source, target, phase, other, slot, form):
         return pltpu.make_async_remote_copy(
@@ -135,26 +144,17 @@
         )
 
     def along_cols(source, target, phase, form):
-        def one(step, carry):
-            col_copy(source, target, phase, lax.rem(col + step, N), col, form).start()
-            return carry
-
-        lax.fori_loop(1, N, one, 0)
+        for offset in COL_OFFSETS[:-1]:
+            col_copy(source, target, phase, col_at(col, offset), col, form).start()
 
     def cols_arrived(source, target, phase, form):
-        def one(step, carry):
-            other = lax.rem(col + N - step, N)
+        for offset in COL_OFFSETS[:-1]:
+            other = col_at(col, offset, -1)
             col_copy(source, target, phase, other, other, form).wait_recv()
-            return carry
-
-        lax.fori_loop(1, N, one, 0)
 
     def cols_left(source, target, phase, form):
-        def one(step, carry):
-            col_copy(source, target, phase, lax.rem(col + step, N), col, form).wait_send()
-            return carry
-
-        lax.fori_loop(1, N, one, 0)
+        for offset in COL_OFFSETS[:-1]:
+            col_copy(source, target, phase, col_at(col, offset), col, form).wait_send()
 
     place = lax.broadcasted_iota(jnp.int32, (K, 1), 0)
     loads[0].wait()
@@ -200,13 +200,10 @@
 
     pass_on(row)
 
-    def relay(step, carry):
-        other = lax.rem(row + N - step, N)
+    for offset in ROW_OFFSETS:
+        other = row_at(row, offset, -1)
         row_copy(site_out, site_in, SITE, other, other).wait_recv()
         pass_on(other)
-        return carry
-
-    lax.fori_loop(1, N, relay, 0)
 
     for half in range(2):
         for part in range(2):
@@ -313,33 +310,71 @@
                 retarded + [s[2 * half], s[2 * half + 1]], axis=0
             ).astype(BF16)
             total = mm(lefts[k, half], right) * STEP_SIZE
-            total = total.reshape(2, N, TILE, LANES).astype(BF16)
-            cb_out[k, 2 * half] = total[0]
-            cb_out[k, 2 * half + 1] = total[1]
-    along_cols(cb_out, cb_in, OUT_B, from_window)
-    cb_in[pl.ds(col, 1)] = cb_out[:, :, pl.ds(col, 1)].reshape(1, 2, 4, TILE, LANES)
-    cols_arrived(cb_out, cb_in, OUT_B, from_window)
-    for m in range(BLOCK):
-        spread[m * BLOCK : (m + 1) * BLOCK, :] = (
-            cb_in[m // 2, m % 2].astype(F32).reshape(BLOCK, LANES)
-        )
-    for half in range(2):
-        for part in range(2):
-            base = part * 16
-            swapped = block_swap(
-                [
-                    spread[pl.ds(base * BLOCK + half * N + q, 16, stride=BLOCK), :]
-                    for q in range(N)
-                ]
+            start = (4 * k + 2 * half) * LANES
+            results[start : start + 2 * LANES, :] = total
+
+    for piece in range(4):
+        swapped = block_swap(
+            [
+                results[pl.ds((q // 2) * LANES + q % 2 + 32 * piece, 16, stride=2), :]
+                for q in range(N)
+            ]
+        )
+        for a in range(N):
+            start = a * N + 4 * piece
+            x_out[start : start + 4] = swapped[a].reshape(4, 4, LANES).astype(BF16)
+    me = row * N + col
+
+    def tile_copy(other_row, other_col):
+        return pltpu.make_async_remote_copy(
+            src_ref=x_out.at[other_row * N + other_col], dst_ref=x_in.at[me],
+            send_sem=tile_sems.at[0], recv_sem=tile_sems.at[1],
+            device_id=(other_row, other_col), device_id_type=MESH,
+        )
+
+    for offset in COL_OFFSETS:
+        other_col = col_at(col, offset)
+
+        def one(i, carry, other_col=other_col):
+            quarter = i // 4
+            dx = jnp.where(quarter == 0, 2, jnp.where(quarter == 3, 0, 2 * quarter - 1))
+            other_row = (
+                ((row // 4 + dx) % 4) * 4
+                + ((row // 2 + 1 - (i // 2) % 2) % 2) * 2
+                + (row + 1 - i % 2) % 2
             )
-            for a in range(N):
-                ca_out[a, half, base : base + 16, :] = swapped[a].astype(BF16)
-    along_rows(ca_out, ca_in, OUT_A)
-    rows_arrived(ca_out, ca_in, OUT_A)
+            tile_copy(other_row, other_col).start()
+            return carry
+
+        lax.fori_loop(0, N - (1 if offset == (0, 0) else 0), one, 0)
+    x_in[pl.ds(me, 1)] = x_out[pl.ds(me, 1)]
+
+    place = lax.broadcasted_iota(jnp.int32, (K, 1), 0)
+    member, device = place // (N * N), place % (N * N)
+    perm[...] = one_hot(
+        device // N + N * (2 * (device % N) + member) == momentum_map[...]
+    )
+    part, early, late = (place // CELLS) % 4, (place // TILE) % TILE, place % TILE
+    lane = (late // 2) * LANES + ((member * 4 + part) * 2 + late % 2) * TILE + early
+    select[...] = one_hot(lane == lax.broadcasted_iota(jnp.int32, (1, K), 1))
+    everyone = pl.ds(0, N * N - 1)
+    pltpu.make_async_copy(x_in.at[everyone], x_in.at[everyone], tile_sems.at[1]).wait()
+    for d in range(N * N):
+        spread[4 * d : 4 * d + 4, :] = x_in[d].astype(F32)
+    rows = jnp.concatenate(
+        [spread[pl.ds(i, N * N, stride=4), :] for i in range(4)], axis=1
+    ).astype(BF16)
+    cells = mm(select[...], rows, NT).astype(BF16)
+    cells = jnp.concatenate([cells[: K // 2], cells[K // 2 :]], axis=1)
+    final = mm(cells, perm[...]).astype(BF16)
     for half, out in enumerate((out_lesser, out_greater)):
-        full = ca_in[:, half].reshape(K, LANES)
-        cells = mm(swap, full, NT).astype(BF16)
-        out[...] = mm(cells, perm[...]).reshape(2, TILE, TILE, K).astype(BF16)
+        out[...] = (
+            final[half * 2 * CELLS : (half + 1) * 2 * CELLS]
+            .astype(F32)
+            .reshape(2, TILE, TILE, K)
+            .astype(BF16)
+        )
+    pltpu.make_async_copy(x_out.at[everyone], x_out.at[everyone], tile_sems.at[0]).wait()
 
     def passed_on(step, carry):
         other = lax.rem(row + step, N)
@@ -356,8 +391,6 @@
     cols_left(gb_out, gb_in, GREEN_B, to_window)
     rows_left(y_out, y_in, INNER)
     cols_left(s_out, s_in, SIGMA, plain)
-    cols_left(cb_out, cb_in, OUT_B, from_window)
-    rows_left(ca_out, ca_in, OUT_A)
 
 
 def sites_of(block):
@@ -430,10 +463,14 @@
             wide, wide, wide, wide,
             by_row, by_row, by_col, window,
             pltpu.VMEM((2, 2, 2 * LANES, 4 * LANES), BF16),
-            window, by_col, by_row, by_row,
+            pltpu.VMEM((2 * K, LANES), F32),
+            pltpu.VMEM((K, K), BF16),
+            pltpu.VMEM((N * N, 4, LANES), BF16),
+            pltpu.VMEM((N * N, 4, LANES), BF16),
             pltpu.SemaphoreType.DMA((6,)),
-            pltpu.SemaphoreType.DMA((8, N)),
-            pltpu.SemaphoreType.DMA((8, N)),
+            pltpu.SemaphoreType.DMA((6, N)),
+            pltpu.SemaphoreType.DMA((6, N)),
+            pltpu.SemaphoreType.DMA((2,)),
         ],
         compiler_params=pltpu.CompilerParams(
             collective_id=0, has_side_effects=True, vmem_limit_bytes=67_043_328

time: 67.2 us -> 61.8 us (0.920)
  Pallas kernels: 63.5 us -> 58.2 us
    pallas_call x1, Pallas kernels: 63.5 us -> 58.2 us  [body(): pl.pallas_call(kernel, out_shape=(tile, tile), in_specs=[pl.BlockSpec(mem...]
where the time goes in v2:
time: 61.8 us; the launch traced here: 61.7 us
  Pallas kernels  58.2 us (94%)
  local copies, waits for them, and re-layouts  2.26 us (4%)
  between operations  1.29 us (2%)
    pallas_call x1, Pallas kernels, body(): pl.pallas_call(kernel, out_shape=(tile, tile), in_specs=[pl.BlockSpec(mem...  58.2 us
    unnamed x4, local copies, waits for them, and re-layouts  2.26 us

profile of v2, /device:TPU:1, one launch (start us, length us, event | category | flops | bytes accessed | tf_op | source)
XLA Modules:
  0.0 61.7 jit_solution(1997141164868019007)
XLA Ops:
  1.3 58.2 %shard_map.86 = (bf16[2,8,8,512]{3,2,1,0:T(8,128)(2,1)}, bf16[2,8,8,512]{3,2,1,0:T(8,128)(2,1)}) custom-call(s32[1]{0:T(128)S(6)} %copy.11.offset_ref, s32[1,512]{1,0:T(1,128)} %bitcast.1, bf16[2,8,8,512]{3,2,1,0:T(8,128)(2,1)} %lesser_hbm.1, bf16[2,8,8,512]{3,2,1,0:T(8,128)(2,1)} %greater_hbm.1, bf16[512,1024]{1,0:T(8,128)(2,1)} %constant.6.clone.table_hbm, ...), custom_call_target="tpu_custom_call" | custom-call | tf_op jit(solution)/shard_map/pallas_call | solution.py:447
  59.4 0.0 copy-start
  59.4 1.6 %copy.12 = bf16[2,8,8,512]{3,2,1,0:T(8,128)(2,1)} copy(bf16[2,8,8,512]{3,2,1,0:T(8,128)(2,1)} %get-tuple-element.4) | data formatting | bytes 262144
  61.1 0.0 copy-done
  61.1 0.7 %copy.13 = bf16[2,8,8,512]{3,2,1,0:T(8,128)(2,1)} copy(bf16[2,8,8,512]{3,2,1,0:T(8,128)(2,1)S(1)} %copy-done) | data formatting | bytes 262144
Async XLA Ops:
  59.4 1.6 %copy-start = (bf16[2,8,8,512]{3,2,1,0:T(8,128)(2,1)S(1)}, bf16[2,8,8,512]{3,2,1,0:T(8,128)(2,1)}, u32[]{:S(2)}) copy-start(bf16[2,8,8,512]{3,2,1,0:T(8,128)(2,1)} %get-tuple-element.5) | copy-start | bytes 393220

commit v3 on v2

--- a/solution.py
+++ b/solution.py
@@ -96,8 +96,8 @@
                 (lesser_hbm, green.at[0]),
                 (greater_hbm, green.at[1]),
                 (table_hbm, table),
+                (outer_hbm, outer),
                 (inner_hbm.at[row], inner),
-                (outer_hbm, outer),
             )
         )
     ]
@@ -167,27 +167,35 @@
         & (r % TILE == (c // TILE) % TILE)
     )
 
-    for load in loads[1:]:
-        load.wait()
+    loads[1].wait()
+    loads[2].wait()
     turned = []
+    pairs = []
     for half in range(2):
         natural = green[half].astype(F32).reshape(2 * CELLS, K).astype(BF16)
         turned.append(mm(swap, natural).astype(BF16))
-        ordered = mm(turned[half], perm[...], NT)
-        g_re, g_im = ordered[:CELLS], ordered[CELLS:]
-        pairs = jnp.concatenate(
-            [jnp.concatenate([g_re, -g_im], axis=1), jnp.concatenate([g_im, g_re], axis=1)],
-            axis=0,
-        ).astype(BF16)
-        sites = mm(table[...], pairs, NT) * NORM
-        site_out[:, half] = sites.reshape(N, BLOCK, LANES).astype(BF16)
+    turned = jnp.concatenate(turned, axis=0)
+    ordered = mm(turned, perm[...], NT)
+    for half in range(2):
+        g_re = ordered[2 * half * CELLS : (2 * half + 1) * CELLS]
+        g_im = ordered[(2 * half + 1) * CELLS : (2 * half + 2) * CELLS]
+        pairs.append(jnp.concatenate([g_re, -g_im], axis=1))
+        pairs.append(jnp.concatenate([g_im, g_re], axis=1))
+    pairs = jnp.concatenate(pairs, axis=0).astype(BF16)
+    loads[3].wait()
+    sites = mm(table[...], pairs, NT) * NORM
+    for half in range(2):
+        site_out[:, half] = (
+            sites[:, half * LANES : (half + 1) * LANES].reshape(N, BLOCK, LANES).astype(BF16)
+        )
 
     pl.semaphore_wait(barrier, 2 * (N - 1))
     along_rows(site_out, site_in, SITE)
-    for half in range(2):
-        spectral = mm(perm[...], turned[half], NT)
-        ga_out[:, half] = spectral.reshape(N, BLOCK, LANES).astype(BF16)
-    along_rows(ga_out, ga_in, GREEN_A)
+    spectral = mm(perm[...], turned, NT)
+    for half in range(2):
+        ga_out[:, half] = (
+            spectral[:, half * LANES : (half + 1) * LANES].reshape(N, BLOCK, LANES).astype(BF16)
+        )
 
     def pass_on(other):
         @pl.when(other != col)
@@ -204,6 +212,7 @@
         other = row_at(row, offset, -1)
         row_copy(site_out, site_in, SITE, other, other).wait_recv()
         pass_on(other)
+    along_rows(ga_out, ga_in, GREEN_A)
 
     for half in range(2):
         for part in range(2):
@@ -228,7 +237,6 @@
     for m in range(BLOCK):
         picked = spread[pl.ds(m, BLOCK, stride=BLOCK), :]
         gb_out[m // 2, m % 2] = picked.reshape(4, TILE, LANES).astype(BF16)
-    along_cols(gb_out, gb_in, GREEN_B, to_window)
     gb_in[:, :, pl.ds(col, 1)] = gb_out[pl.ds(col, 1)].reshape(2, 4, 1, TILE, LANES)
 
     steps = lax.broadcasted_iota(jnp.int32, (TILE, LANES), 1)
@@ -247,6 +255,7 @@
     edge = (fc // 16) * 16 + jnp.where(first_run, (16 - fc % 16) % 16, 15 - fc % 16)
     flip = one_hot(fr == inside + jnp.where(row == 0, 1, 0) * (edge - inside))
 
+    along_cols(gb_out, gb_in, GREEN_B, to_window)
     cols_arrived(site_in, mirror_in, MIRROR, plain)
     spread[...] = mm(mirror_in[...].reshape(2 * K, LANES), swap)
     for half in range(2):
@@ -273,6 +282,7 @@
         selves[at : at + BLOCK] = self_re.astype(BF16)
         selves[at + BLOCK : at + 2 * BLOCK] = self_im.astype(BF16)
     doubled = jnp.concatenate([selves[...], selves[...]], axis=0)
+    loads[5].wait()
     y_out[...] = mm(inner[...], doubled).reshape(N, TILE, WIDE).astype(BF16)
     along_rows(y_out, y_in, INNER)
 
@@ -291,6 +301,7 @@
                     blocks, axis=1
                 ).astype(BF16)
 
+    loads[4].wait()
     rows_arrived(y_out, y_in, INNER)
     arrived = y_in[...].astype(F32).reshape(LANES, WIDE).astype(BF16)
     sigma = mm(outer[...], jnp.concatenate([arrived, arrived], axis=0)) * NORM
@@ -473,11 +484,17 @@
             pltpu.SemaphoreType.DMA((2,)),
         ],
         compiler_params=pltpu.CompilerParams(
-            collective_id=0, has_side_effects=True, vmem_limit_bytes=67_043_328
+            collective_id=0, has_side_effects=True, vmem_limit_bytes=32 * 1024 * 1024
         ),
     )(
-        time_offset, lattice_map.reshape(1, K), green_lesser, green_greater,
-        *(jnp.asarray(value) for value in constants()),
+        time_offset,
+        *(
+            pltpu.with_memory_space_constraint(value, pltpu.MemorySpace.HBM)
+            for value in (
+                lattice_map.reshape(1, K), green_lesser, green_greater,
+                *(jnp.asarray(value) for value in constants()),
+            )
+        ),
     )
 
 

time: 61.8 us -> 58.8 us (0.951)
  Pallas kernels: 58.2 us -> 56.1 us
  local copies, waits for them, and re-layouts: 2.26 us -> 1.31 us
    pallas_call x1, Pallas kernels: 58.2 us -> 56.1 us  [body(): pl.pallas_call(kernel, out_shape=(tile, tile), in_specs=[pl.BlockSpec(mem...]
    unnamed x4 -> x2, local copies, waits for them, and re-layouts: 2.26 us -> 1.31 us
where the time goes in v3:
time: 58.8 us; the launch traced here: 58.7 us
  Pallas kernels  56.1 us (95%)
  local copies, waits for them, and re-layouts  1.31 us (2%)
  between operations  1.29 us (2%)
    pallas_call x1, Pallas kernels, body(): pl.pallas_call(kernel, out_shape=(tile, tile), in_specs=[pl.BlockSpec(mem...  56.1 us
    unnamed x2, local copies, waits for them, and re-layouts  1.31 us

profile of v3, /device:TPU:1, one launch (start us, length us, event | category | flops | bytes accessed | tf_op | source)
XLA Modules:
  0.0 58.7 jit_solution(14634328122964341999)
XLA Ops:
  1.3 56.1 %shard_map.86 = (bf16[2,8,8,512]{3,2,1,0:T(8,128)(2,1)S(1)}, bf16[2,8,8,512]{3,2,1,0:T(8,128)(2,1)S(1)}) custom-call(s32[1]{0:T(128)S(6)} %copy.11.offset_ref, s32[1,512]{1,0:T(1,128)} %bitcast.1, bf16[2,8,8,512]{3,2,1,0:T(8,128)(2,1)} %lesser_hbm.1, bf16[2,8,8,512]{3,2,1,0:T(8,128)(2,1)} %greater_hbm.1, bf16[512,1024]{1,0:T(8,128)(2,1)} %constant.6.clone.table_hbm, ...), custom_call_target="tpu_custom_call" | custom-call | tf_op jit(solution)/shard_map/pallas_call | solution.py:458
  57.4 0.7 %copy.12 = bf16[2,8,8,512]{3,2,1,0:T(8,128)(2,1)} copy(bf16[2,8,8,512]{3,2,1,0:T(8,128)(2,1)S(1)} %get-tuple-element.4) | data formatting | bytes 262144
  58.0 0.7 %copy.13 = bf16[2,8,8,512]{3,2,1,0:T(8,128)(2,1)} copy(bf16[2,8,8,512]{3,2,1,0:T(8,128)(2,1)S(1)} %get-tuple-element.5) | data formatting | bytes 262144

commit v4 on v3

--- a/solution.py
+++ b/solution.py
@@ -27,7 +27,7 @@
 NT = (((1,), (1,)), ((), ()))
 NN = (((1,), (0,)), ((), ()))
 
-SITE, MIRROR, INNER, SIGMA, GREEN_A, GREEN_B = range(6)
+SITE, MIRROR, GREEN_A, GREEN_B, INNER, SIGMA = 0, 1, 2, 3, (4, 5), (6, 7)
 
 ROW_OFFSETS = sorted(
     ((x, y, c) for x in (2, 1, -1, 0) for y in (1, 0) for c in (0, 1)),
@@ -79,7 +79,7 @@
 def kernel(
     offset_ref, map_hbm, lesser_hbm, greater_hbm, table_hbm, inner_hbm, outer_hbm,
     out_lesser, out_greater,
-    momentum_map, green, table, inner, outer, perm, spread, own, mirror, selves,
+    momentum_map, green, table, inner, outer, perm, spread, own, mirror,
     site_out, site_in, mirror_in, y_out, y_in, s_out, s_in,
     ga_out, ga_in, gb_out, gb_in, lefts, results, select, x_out, x_in,
     load_sems, send_sems, recv_sems, tile_sems,
@@ -112,29 +112,38 @@
             barrier, inc=1, device_id=(row_at(row, offset), col), device_id_type=MESH
         )
 
-    def row_copy(source, target, phase, other, slot):
+    def plain(ref, i):
+        return ref.at[i]
+
+    def in_window(ref, i):
+        return ref.at[:, :, i]
+
+    def lane_half(part):
+        return lambda ref, i: ref.at[i, :, pl.ds(part * (WIDE // 2), WIDE // 2)]
+
+    to_window = (plain, in_window)
+    plain = (plain, plain)
+    lane_halves = [(lane_half(part), lane_half(part)) for part in range(2)]
+
+    def row_copy(source, target, phase, other, slot, form=plain):
         return pltpu.make_async_remote_copy(
-            src_ref=source.at[other], dst_ref=target.at[slot],
+            src_ref=form[0](source, other), dst_ref=form[1](target, slot),
             send_sem=send_sems.at[phase, other], recv_sem=recv_sems.at[phase, slot],
             device_id=(other, col), device_id_type=MESH,
         )
 
-    def along_rows(source, target, phase):
+    def along_rows(source, target, phase, form=plain):
         for offset in ROW_OFFSETS:
-            row_copy(source, target, phase, row_at(row, offset), row).start()
-        target[pl.ds(row, 1)] = source[pl.ds(row, 1)]
-
-    def rows_arrived(source, target, phase):
+            row_copy(source, target, phase, row_at(row, offset), row, form).start()
+
+    def rows_arrived(source, target, phase, form=plain):
         for offset in ROW_OFFSETS:
             other = row_at(row, offset, -1)
-            row_copy(source, target, phase, other, other).wait_recv()
-
-    def rows_left(source, target, phase):
+            row_copy(source, target, phase, other, other, form).wait_recv()
+
+    def rows_left(source, target, phase, form=plain):
         for offset in ROW_OFFSETS:
-            row_copy(source, target, phase, row_at(row, offset), row).wait_send()
-
-    plain = (lambda ref, i: ref.at[i], lambda ref, i: ref.at[i])
-    to_window = (lambda ref, i: ref.at[i], lambda ref, i: ref.at[:, :, i])
+            row_copy(source, target, phase, row_at(row, offset), row, form).wait_send()
 
     def col_copy(source, target, phase, other, slot, form):
         return pltpu.make_async_remote_copy(
@@ -169,13 +178,11 @@
 
     loads[1].wait()
     loads[2].wait()
-    turned = []
     pairs = []
-    for half in range(2):
-        natural = green[half].astype(F32).reshape(2 * CELLS, K).astype(BF16)
-        turned.append(mm(swap, natural).astype(BF16))
-    turned = jnp.concatenate(turned, axis=0)
-    ordered = mm(turned, perm[...], NT)
+    natural = jnp.concatenate(
+        [green[half].astype(F32).reshape(2 * CELLS, K) for half in range(2)], axis=0
+    ).astype(BF16)
+    ordered = mm(natural, perm[...], NT)
     for half in range(2):
         g_re = ordered[2 * half * CELLS : (2 * half + 1) * CELLS]
         g_im = ordered[(2 * half + 1) * CELLS : (2 * half + 2) * CELLS]
@@ -191,7 +198,8 @@
 
     pl.semaphore_wait(barrier, 2 * (N - 1))
     along_rows(site_out, site_in, SITE)
-    spectral = mm(perm[...], turned, NT)
+    site_in[pl.ds(row, 1)] = site_out[pl.ds(row, 1)]
+    spectral = mm(perm[...], natural, NT)
     for half in range(2):
         ga_out[:, half] = (
             spectral[:, half * LANES : (half + 1) * LANES].reshape(N, BLOCK, LANES).astype(BF16)
@@ -213,24 +221,28 @@
         row_copy(site_out, site_in, SITE, other, other).wait_recv()
         pass_on(other)
     along_rows(ga_out, ga_in, GREEN_A)
-
-    for half in range(2):
-        for part in range(2):
-            base = part * 16
-            swapped = block_swap(
-                [site_in[a, half, base : base + 16, :].astype(F32) for a in range(N)]
-            )
-            for q in range(N):
-                at, lane = (q // TILE) * BLOCK + base, (q % TILE) * LANES
-                own[half, at : at + 16, lane : lane + LANES] = swapped[q].astype(BF16)
+    ga_in[pl.ds(row, 1)] = ga_out[pl.ds(row, 1)]
+
+    def pieces(ref, half, base):
+        return [
+            ref[pl.ds(i * 2 * BLOCK + half * BLOCK + base, 16), :] for i in range(N)
+        ]
+
+    def to_rows(target, half, base, swapped):
+        for q in range(N):
+            at, lane = (q // TILE) * BLOCK + base, (q % TILE) * LANES
+            target[half, at : at + 16, lane : lane + LANES] = swapped[q].astype(BF16)
+
+    spread[...] = mm(site_in[...].reshape(2 * K, LANES), swap)
+    for half in range(2):
+        for base in (0, 16):
+            to_rows(own, half, base, block_swap(pieces(spread, half, base)))
 
     rows_arrived(ga_out, ga_in, GREEN_A)
-    for half in range(2):
-        for part in range(2):
-            base = part * 16
-            swapped = block_swap(
-                [ga_in[a, half, base : base + 16, :].astype(F32) for a in range(N)]
-            )
+    results[...] = mm(ga_in[...].reshape(2 * K, LANES), swap)
+    for half in range(2):
+        for base in (0, 16):
+            swapped = block_swap(pieces(results, half, base))
             for q in range(N):
                 start = (half * N + q) * BLOCK + base
                 spread[start : start + 16, :] = swapped[q]
@@ -257,34 +269,29 @@
 
     along_cols(gb_out, gb_in, GREEN_B, to_window)
     cols_arrived(site_in, mirror_in, MIRROR, plain)
-    spread[...] = mm(mirror_in[...].reshape(2 * K, LANES), swap)
-    for half in range(2):
-        for part in range(2):
-            base = part * 16
-            swapped = block_swap(
-                [
-                    spread[pl.ds(b * 2 * BLOCK + half * BLOCK + base, 16), :]
-                    for b in range(N)
-                ]
-            )
-            for q in range(N):
-                at, lane = (q // TILE) * BLOCK + base, (q % TILE) * LANES
-                mirror[half, at : at + 16, lane : lane + LANES] = swapped[q].astype(BF16)
-    for half in range(2):
-        first_re, first_im = own[half, :BLOCK].astype(F32), own[half, BLOCK:].astype(F32)
-        other = mm(flip, mirror[1 - half])
-        other_re, other_im = other[:BLOCK], other[BLOCK:]
-        square_re = first_re * first_re - first_im * first_im
-        square_im = 2.0 * first_re * first_im
-        self_re = coupling * (square_re * other_re - square_im * other_im)
-        self_im = coupling * (square_re * other_im + square_im * other_re)
-        at = half * 2 * BLOCK
-        selves[at : at + BLOCK] = self_re.astype(BF16)
-        selves[at + BLOCK : at + 2 * BLOCK] = self_im.astype(BF16)
-    doubled = jnp.concatenate([selves[...], selves[...]], axis=0)
+    for half in range(2):
+        for base in (0, 16):
+            arrived = [mirror_in[b, half, base : base + 16, :].astype(F32) for b in range(N)]
+            to_rows(mirror, half, base, block_swap(arrived))
     loads[5].wait()
-    y_out[...] = mm(inner[...], doubled).reshape(N, TILE, WIDE).astype(BF16)
-    along_rows(y_out, y_in, INNER)
+    for part in range(2):
+        lanes = slice(part * (WIDE // 2), (part + 1) * (WIDE // 2))
+        weight = coupling[:, lanes]
+        selves = []
+        for half in range(2):
+            first_re = own[half, :BLOCK, lanes].astype(F32)
+            first_im = own[half, BLOCK:, lanes].astype(F32)
+            other = mm(flip, mirror[1 - half, :, lanes])
+            other_re, other_im = other[:BLOCK], other[BLOCK:]
+            square_re = first_re * first_re - first_im * first_im
+            square_im = 2.0 * first_re * first_im
+            selves.append(weight * (square_re * other_re - square_im * other_im))
+            selves.append(weight * (square_re * other_im + square_im * other_re))
+        selves = jnp.concatenate(selves, axis=0).astype(BF16)
+        terms = mm(inner[...], jnp.concatenate([selves, selves], axis=0))
+        y_out[:, :, lanes] = terms.reshape(N, TILE, WIDE // 2).astype(BF16)
+        along_rows(y_out, y_in, INNER[part], lane_halves[part])
+    y_in[pl.ds(row, 1)] = y_out[pl.ds(row, 1)]
 
     down = lax.broadcasted_iota(jnp.int32, (LANES, LANES), 0)
     across = lax.broadcasted_iota(jnp.int32, (LANES, LANES), 1)
@@ -302,17 +309,22 @@
                 ).astype(BF16)
 
     loads[4].wait()
-    rows_arrived(y_out, y_in, INNER)
-    arrived = y_in[...].astype(F32).reshape(LANES, WIDE).astype(BF16)
-    sigma = mm(outer[...], jnp.concatenate([arrived, arrived], axis=0)) * NORM
-    s_out[...] = sigma.reshape(N, TILE, WIDE).astype(BF16)
-    along_cols(s_out, s_in, SIGMA, plain)
+    for part in range(2):
+        lanes = slice(part * (WIDE // 2), (part + 1) * (WIDE // 2))
+        rows_arrived(y_out, y_in, INNER[part], lane_halves[part])
+        arrived = y_in[:, :, lanes].astype(F32).reshape(LANES, WIDE // 2).astype(BF16)
+        sigma = mm(outer[...], jnp.concatenate([arrived, arrived], axis=0)) * NORM
+        s_out[:, :, lanes] = sigma.reshape(N, TILE, WIDE // 2).astype(BF16)
+        along_cols(s_out, s_in, SIGMA[part], lane_halves[part])
     s_in[pl.ds(col, 1)] = s_out[pl.ds(col, 1)]
-    cols_arrived(s_out, s_in, SIGMA, plain)
-    for b in range(N):
-        for t in range(TILE):
-            start = (b * TILE + t) * TILE
-            spread[start : start + TILE, :] = s_in[b, :, t * LANES : (t + 1) * LANES].astype(F32)
+    for part in range(2):
+        cols_arrived(s_out, s_in, SIGMA[part], lane_halves[part])
+        for b in range(N):
+            for t in range(part * TILE // 2, (part + 1) * TILE // 2):
+                start = (b * TILE + t) * TILE
+                spread[start : start + TILE, :] = s_in[
+                    b, :, t * LANES : (t + 1) * LANES
+                ].astype(F32)
     for k in range(2):
         s = [spread[pl.ds(4 * k + i, LANES, stride=TILE), :] for i in range(4)]
         retarded = [jnp.where(down <= across, s[2 + i] - s[i], 0.0) for i in range(2)]
@@ -400,8 +412,9 @@
     rows_left(site_out, site_in, SITE)
     rows_left(ga_out, ga_in, GREEN_A)
     cols_left(gb_out, gb_in, GREEN_B, to_window)
-    rows_left(y_out, y_in, INNER)
-    cols_left(s_out, s_in, SIGMA, plain)
+    for part in range(2):
+        rows_left(y_out, y_in, INNER[part], lane_halves[part])
+        cols_left(s_out, s_in, SIGMA[part], lane_halves[part])
 
 
 def sites_of(block):
@@ -469,7 +482,6 @@
             pltpu.VMEM((K, K), BF16),
             pltpu.VMEM((2 * K, LANES), F32),
             halves, halves,
-            pltpu.VMEM((LANES, WIDE), BF16),
             by_row, by_row, by_row,
             wide, wide, wide, wide,
             by_row, by_row, by_col, window,
@@ -479,8 +491,8 @@
             pltpu.VMEM((N * N, 4, LANES), BF16),
             pltpu.VMEM((N * N, 4, LANES), BF16),
             pltpu.SemaphoreType.DMA((6,)),
-            pltpu.SemaphoreType.DMA((6, N)),
-            pltpu.SemaphoreType.DMA((6, N)),
+            pltpu.SemaphoreType.DMA((8, N)),
+            pltpu.SemaphoreType.DMA((8, N)),
             pltpu.SemaphoreType.DMA((2,)),
         ],
         compiler_params=pltpu.CompilerParams(

time: 58.8 us -> 60.4 us (1.027)
  Pallas kernels: 56.1 us -> 57.6 us
    pallas_call x1, Pallas kernels: 56.1 us -> 57.6 us  [body(): pl.pallas_call(kernel, out_shape=(tile, tile), in_specs=[pl.BlockSpec(mem...]
where the time goes in v4:
time: 60.4 us; the launch traced here: 60.2 us
  Pallas kernels  57.6 us (95%)
  local copies, waits for them, and re-layouts  1.31 us (2%)
  between operations  1.29 us (2%)
    pallas_call x1, Pallas kernels, body(): pl.pallas_call(kernel, out_shape=(tile, tile), in_specs=[pl.BlockSpec(mem...  57.6 us
    unnamed x2, local copies, waits for them, and re-layouts  1.31 us

profile of v4, /device:TPU:1, one launch (start us, length us, event | category | flops | bytes accessed | tf_op | source)
XLA Modules:
  0.0 60.2 jit_solution(2274213018404578451)
XLA Ops:
  1.3 57.6 %shard_map.86 = (bf16[2,8,8,512]{3,2,1,0:T(8,128)(2,1)S(1)}, bf16[2,8,8,512]{3,2,1,0:T(8,128)(2,1)S(1)}) custom-call(s32[1]{0:T(128)S(6)} %copy.11.offset_ref, s32[1,512]{1,0:T(1,128)} %bitcast.1, bf16[2,8,8,512]{3,2,1,0:T(8,128)(2,1)} %lesser_hbm.1, bf16[2,8,8,512]{3,2,1,0:T(8,128)(2,1)} %greater_hbm.1, bf16[512,1024]{1,0:T(8,128)(2,1)} %constant.6.clone.table_hbm, ...), custom_call_target="tpu_custom_call" | custom-call | tf_op jit(solution)/shard_map/pallas_call | solution.py:471
  58.9 0.7 %copy.12 = bf16[2,8,8,512]{3,2,1,0:T(8,128)(2,1)} copy(bf16[2,8,8,512]{3,2,1,0:T(8,128)(2,1)S(1)} %get-tuple-element.4) | data formatting | bytes 262144
  59.6 0.7 %copy.13 = bf16[2,8,8,512]{3,2,1,0:T(8,128)(2,1)} copy(bf16[2,8,8,512]{3,2,1,0:T(8,128)(2,1)S(1)} %get-tuple-element.5) | data formatting | bytes 262144

commit v5 on v3

--- a/solution.py
+++ b/solution.py
@@ -212,7 +212,8 @@
         other = row_at(row, offset, -1)
         row_copy(site_out, site_in, SITE, other, other).wait_recv()
         pass_on(other)
-    along_rows(ga_out, ga_in, GREEN_A)
+        row_copy(ga_out, ga_in, GREEN_A, row_at(row, offset), row).start()
+    ga_in[pl.ds(row, 1)] = ga_out[pl.ds(row, 1)]
 
     for half in range(2):
         for part in range(2):
@@ -343,21 +344,15 @@
             device_id=(other_row, other_col), device_id_type=MESH,
         )
 
-    for offset in COL_OFFSETS:
-        other_col = col_at(col, offset)
-
-        def one(i, carry, other_col=other_col):
-            quarter = i // 4
-            dx = jnp.where(quarter == 0, 2, jnp.where(quarter == 3, 0, 2 * quarter - 1))
-            other_row = (
-                ((row // 4 + dx) % 4) * 4
-                + ((row // 2 + 1 - (i // 2) % 2) % 2) * 2
-                + (row + 1 - i % 2) % 2
-            )
-            tile_copy(other_row, other_col).start()
-            return carry
-
-        lax.fori_loop(0, N - (1 if offset == (0, 0) else 0), one, 0)
+    row_ids = [row_at(row, offset) for offset in ROW_OFFSETS] + [row]
+    col_ids = [col_at(col, offset) for offset in COL_OFFSETS]
+    row_far = [abs(o[0]) + o[1] + 0.2 * o[2] for o in ROW_OFFSETS] + [0.0]
+    col_far = [abs(o[1]) + 2 * o[0] for o in COL_OFFSETS]
+    order = sorted(
+        ((i, j) for j in range(N) for i in range(N)), key=lambda p: -(row_far[p[0]] + col_far[p[1]])
+    )[:-1]
+    for i, j in order:
+        tile_copy(row_ids[i], col_ids[j]).start()
     x_in[pl.ds(me, 1)] = x_out[pl.ds(me, 1)]
 
     place = lax.broadcasted_iota(jnp.int32, (K, 1), 0)

time: 58.8 us -> 55.6 us (0.946)
  Pallas kernels: 56.1 us -> 52.9 us
    pallas_call x1, Pallas kernels: 56.1 us -> 52.9 us  [body(): pl.pallas_call(kernel, out_shape=(tile, tile), in_specs=[pl.BlockSpec(mem...]
where the time goes in v5:
time: 55.6 us; the launch traced here: 55.5 us
  Pallas kernels  52.9 us (95%)
  local copies, waits for them, and re-layouts  1.31 us (2%)
  between operations  1.29 us (2%)
    pallas_call x1, Pallas kernels, body(): pl.pallas_call(kernel, out_shape=(tile, tile), in_specs=[pl.BlockSpec(mem...  52.9 us
    unnamed x2, local copies, waits for them, and re-layouts  1.31 us

profile of v5, /device:TPU:1, one launch (start us, length us, event | category | flops | bytes accessed | tf_op | source)
XLA Modules:
  0.0 55.5 jit_solution(3272053396910901214)
XLA Ops:
  1.3 52.9 %shard_map.86 = (bf16[2,8,8,512]{3,2,1,0:T(8,128)(2,1)S(1)}, bf16[2,8,8,512]{3,2,1,0:T(8,128)(2,1)S(1)}) custom-call(s32[1]{0:T(128)S(6)} %copy.11.offset_ref, s32[1,512]{1,0:T(1,128)} %bitcast.1, bf16[2,8,8,512]{3,2,1,0:T(8,128)(2,1)} %lesser_hbm.1, bf16[2,8,8,512]{3,2,1,0:T(8,128)(2,1)} %greater_hbm.1, bf16[512,1024]{1,0:T(8,128)(2,1)} %constant.6.clone.table_hbm, ...), custom_call_target="tpu_custom_call" | custom-call | tf_op jit(solution)/shard_map/pallas_call | solution.py:453
  54.2 0.7 %copy.12 = bf16[2,8,8,512]{3,2,1,0:T(8,128)(2,1)} copy(bf16[2,8,8,512]{3,2,1,0:T(8,128)(2,1)S(1)} %get-tuple-element.4) | data formatting | bytes 262144
  54.9 0.7 %copy.13 = bf16[2,8,8,512]{3,2,1,0:T(8,128)(2,1)} copy(bf16[2,8,8,512]{3,2,1,0:T(8,128)(2,1)S(1)} %get-tuple-element.5) | data formatting | bytes 262144

commit v6 on v5

--- a/solution.py
+++ b/solution.py
@@ -87,6 +87,10 @@
     row = lax.axis_index("trow")
     col = lax.axis_index("tcol")
     barrier = pltpu.get_barrier_semaphore()
+    row_to = [row_at(row, offset) for offset in ROW_OFFSETS]
+    row_from = [row_at(row, offset, -1) for offset in ROW_OFFSETS]
+    col_to = [col_at(col, offset) for offset in COL_OFFSETS[:-1]]
+    col_from = [col_at(col, offset, -1) for offset in COL_OFFSETS[:-1]]
 
     loads = [
         pltpu.make_async_copy(source, target, load_sems.at[i])
@@ -103,14 +107,10 @@
     ]
     for load in loads:
         load.start()
-    for offset in COL_OFFSETS[:-1]:
-        pl.semaphore_signal(
-            barrier, inc=1, device_id=(row, col_at(col, offset)), device_id_type=MESH
-        )
-    for offset in ROW_OFFSETS:
-        pl.semaphore_signal(
-            barrier, inc=1, device_id=(row_at(row, offset), col), device_id_type=MESH
-        )
+    for other in col_to:
+        pl.semaphore_signal(barrier, inc=1, device_id=(row, other), device_id_type=MESH)
+    for other in row_to:
+        pl.semaphore_signal(barrier, inc=1, device_id=(other, col), device_id_type=MESH)
 
     def row_copy(source, target, phase, other, slot):
         return pltpu.make_async_remote_copy(
@@ -120,18 +120,17 @@
         )
 
     def along_rows(source, target, phase):
-        for offset in ROW_OFFSETS:
-            row_copy(source, target, phase, row_at(row, offset), row).start()
+        for other in row_to:
+            row_copy(source, target, phase, other, row).start()
         target[pl.ds(row, 1)] = source[pl.ds(row, 1)]
 
     def rows_arrived(source, target, phase):
-        for offset in ROW_OFFSETS:
-            other = row_at(row, offset, -1)
+        for other in row_from:
             row_copy(source, target, phase, other, other).wait_recv()
 
     def rows_left(source, target, phase):
-        for offset in ROW_OFFSETS:
-            row_copy(source, target, phase, row_at(row, offset), row).wait_send()
+        for other in row_to:
+            row_copy(source, target, phase, other, row).wait_send()
 
     plain = (lambda ref, i: ref.at[i], lambda ref, i: ref.at[i])
     to_window = (lambda ref, i: ref.at[i], lambda ref, i: ref.at[:, :, i])
@@ -144,17 +143,16 @@
         )
 
     def along_cols(source, target, phase, form):
-        for offset in COL_OFFSETS[:-1]:
-            col_copy(source, target, phase, col_at(col, offset), col, form).start()
+        for other in col_to:
+            col_copy(source, target, phase, other, col, form).start()
 
     def cols_arrived(source, target, phase, form):
-        for offset in COL_OFFSETS[:-1]:
-            other = col_at(col, offset, -1)
+        for other in col_from:
             col_copy(source, target, phase, other, other, form).wait_recv()
 
     def cols_left(source, target, phase, form):
-        for offset in COL_OFFSETS[:-1]:
-            col_copy(source, target, phase, col_at(col, offset), col, form).wait_send()
+        for other in col_to:
+            col_copy(source, target, phase, other, col, form).wait_send()
 
     place = lax.broadcasted_iota(jnp.int32, (K, 1), 0)
     loads[0].wait()
@@ -208,12 +206,10 @@
 
     pass_on(row)
 
-    for offset in ROW_OFFSETS:
-        other = row_at(row, offset, -1)
+    for other in row_from:
         row_copy(site_out, site_in, SITE, other, other).wait_recv()
         pass_on(other)
-        row_copy(ga_out, ga_in, GREEN_A, row_at(row, offset), row).start()
-    ga_in[pl.ds(row, 1)] = ga_out[pl.ds(row, 1)]
+    along_rows(ga_out, ga_in, GREEN_A)
 
     for half in range(2):
         for part in range(2):
@@ -344,8 +340,8 @@
             device_id=(other_row, other_col), device_id_type=MESH,
         )
 
-    row_ids = [row_at(row, offset) for offset in ROW_OFFSETS] + [row]
-    col_ids = [col_at(col, offset) for offset in COL_OFFSETS]
+    row_ids = row_to + [row]
+    col_ids = col_to + [col]
     row_far = [abs(o[0]) + o[1] + 0.2 * o[2] for o in ROW_OFFSETS] + [0.0]
     col_far = [abs(o[1]) + 2 * o[0] for o in COL_OFFSETS]
     order = sorted(
@@ -363,6 +359,22 @@
     part, early, late = (place // CELLS) % 4, (place // TILE) % TILE, place % TILE
     lane = (late // 2) * LANES + ((member * 4 + part) * 2 + late % 2) * TILE + early
     select[...] = one_hot(lane == lax.broadcasted_iota(jnp.int32, (1, K), 1))
+    def passed_on(step, carry):
+        other = lax.rem(row + step, N)
+
+        @pl.when(other != col)
+        def _():
+            col_copy(site_in, mirror_in, MIRROR, other, col, plain).wait_send()
+
+        return carry
+
+    lax.fori_loop(0, N, passed_on, 0)
+    rows_left(site_out, site_in, SITE)
+    rows_left(ga_out, ga_in, GREEN_A)
+    cols_left(gb_out, gb_in, GREEN_B, to_window)
+    rows_left(y_out, y_in, INNER)
+    cols_left(s_out, s_in, SIGMA, plain)
+
     everyone = pl.ds(0, N * N - 1)
     pltpu.make_async_copy(x_in.at[everyone], x_in.at[everyone], tile_sems.at[1]).wait()
     for d in range(N * N):
@@ -381,22 +393,6 @@
             .astype(BF16)
         )
     pltpu.make_async_copy(x_out.at[everyone], x_out.at[everyone], tile_sems.at[0]).wait()
-
-    def passed_on(step, carry):
-        other = lax.rem(row + step, N)
-
-        @pl.when(other != col)
-        def _():
-            col_copy(site_in, mirror_in, MIRROR, other, col, plain).wait_send()
-
-        return carry
-
-    lax.fori_loop(0, N, passed_on, 0)
-    rows_left(site_out, site_in, SITE)
-    rows_left(ga_out, ga_in, GREEN_A)
-    cols_left(gb_out, gb_in, GREEN_B, to_window)
-    rows_left(y_out, y_in, INNER)
-    cols_left(s_out, s_in, SIGMA, plain)
 
 
 def sites_of(block):

time: 55.6 us -> 55.6 us (level)
  no operation moved by 1% of the time
where the time goes in v6:
time: 55.6 us; the launch traced here: 55.5 us
  Pallas kernels  52.9 us (95%)
  local copies, waits for them, and re-layouts  1.31 us (2%)
  between operations  1.29 us (2%)
    pallas_call x1, Pallas kernels, body(): pl.pallas_call(kernel, out_shape=(tile, tile), in_specs=[pl.BlockSpec(mem...  52.9 us
    unnamed x2, local copies, waits for them, and re-layouts  1.31 us

profile of v6, /device:TPU:1, one launch (start us, length us, event | category | flops | bytes accessed | tf_op | source)
XLA Modules:
  0.0 55.5 jit_solution(10262819531059560511)
XLA Ops:
  1.3 52.9 %shard_map.86 = (bf16[2,8,8,512]{3,2,1,0:T(8,128)(2,1)S(1)}, bf16[2,8,8,512]{3,2,1,0:T(8,128)(2,1)S(1)}) custom-call(s32[1]{0:T(128)S(6)} %copy.11.offset_ref, s32[1,512]{1,0:T(1,128)} %bitcast.1, bf16[2,8,8,512]{3,2,1,0:T(8,128)(2,1)} %lesser_hbm.1, bf16[2,8,8,512]{3,2,1,0:T(8,128)(2,1)} %greater_hbm.1, bf16[512,1024]{1,0:T(8,128)(2,1)} %constant.6.clone.table_hbm, ...), custom_call_target="tpu_custom_call" | custom-call | tf_op jit(solution)/shard_map/pallas_call | solution.py:449
  54.2 0.7 %copy.12 = bf16[2,8,8,512]{3,2,1,0:T(8,128)(2,1)} copy(bf16[2,8,8,512]{3,2,1,0:T(8,128)(2,1)S(1)} %get-tuple-element.4) | data formatting | bytes 262144
  54.8 0.7 %copy.13 = bf16[2,8,8,512]{3,2,1,0:T(8,128)(2,1)} copy(bf16[2,8,8,512]{3,2,1,0:T(8,128)(2,1)S(1)} %get-tuple-element.5) | data formatting | bytes 262144

commit v7 on v6

--- a/solution.py
+++ b/solution.py
@@ -133,7 +133,6 @@
             row_copy(source, target, phase, other, row).wait_send()
 
     plain = (lambda ref, i: ref.at[i], lambda ref, i: ref.at[i])
-    to_window = (lambda ref, i: ref.at[i], lambda ref, i: ref.at[:, :, i])
 
     def col_copy(source, target, phase, other, slot, form):
         return pltpu.make_async_remote_copy(
@@ -234,7 +233,7 @@
     for m in range(BLOCK):
         picked = spread[pl.ds(m, BLOCK, stride=BLOCK), :]
         gb_out[m // 2, m % 2] = picked.reshape(4, TILE, LANES).astype(BF16)
-    gb_in[:, :, pl.ds(col, 1)] = gb_out[pl.ds(col, 1)].reshape(2, 4, 1, TILE, LANES)
+    gb_in[pl.ds(col, 1)] = gb_out[pl.ds(col, 1)]
 
     steps = lax.broadcasted_iota(jnp.int32, (TILE, LANES), 1)
     late = lax.broadcasted_iota(jnp.int32, (TILE, LANES), 0) + col * TILE
@@ -252,7 +251,7 @@
     edge = (fc // 16) * 16 + jnp.where(first_run, (16 - fc % 16) % 16, 15 - fc % 16)
     flip = one_hot(fr == inside + jnp.where(row == 0, 1, 0) * (edge - inside))
 
-    along_cols(gb_out, gb_in, GREEN_B, to_window)
+    along_cols(gb_out, gb_in, GREEN_B, plain)
     cols_arrived(site_in, mirror_in, MIRROR, plain)
     spread[...] = mm(mirror_in[...].reshape(2 * K, LANES), swap)
     for half in range(2):
@@ -285,9 +284,12 @@
 
     down = lax.broadcasted_iota(jnp.int32, (LANES, LANES), 0)
     across = lax.broadcasted_iota(jnp.int32, (LANES, LANES), 1)
-    cols_arrived(gb_out, gb_in, GREEN_B, to_window)
+    cols_arrived(gb_out, gb_in, GREEN_B, plain)
     for k in range(2):
-        g = [gb_in[k, i].astype(F32).reshape(LANES, LANES) for i in range(4)]
+        g = [
+            jnp.concatenate([gb_in[b, k, i].astype(F32) for b in range(N)], axis=0)
+            for i in range(4)
+        ]
         advanced = [jnp.where(across <= down, g[i] - g[2 + i], 0.0) for i in range(2)]
         for half in range(2):
             g_re, g_im = g[2 * half], g[2 * half + 1]
@@ -305,6 +307,14 @@
     s_out[...] = sigma.reshape(N, TILE, WIDE).astype(BF16)
     along_cols(s_out, s_in, SIGMA, plain)
     s_in[pl.ds(col, 1)] = s_out[pl.ds(col, 1)]
+    place = lax.broadcasted_iota(jnp.int32, (K, 1), 0)
+    member, device = place // (N * N), place % (N * N)
+    perm[...] = one_hot(
+        device // N + N * (2 * (device % N) + member) == momentum_map[...]
+    )
+    part, early, late = (place // CELLS) % 4, (place // TILE) % TILE, place % TILE
+    lane = (late // 2) * LANES + ((member * 4 + part) * 2 + late % 2) * TILE + early
+    select[...] = one_hot(lane == lax.broadcasted_iota(jnp.int32, (1, K), 1))
     cols_arrived(s_out, s_in, SIGMA, plain)
     for b in range(N):
         for t in range(TILE):
@@ -351,14 +361,6 @@
         tile_copy(row_ids[i], col_ids[j]).start()
     x_in[pl.ds(me, 1)] = x_out[pl.ds(me, 1)]
 
-    place = lax.broadcasted_iota(jnp.int32, (K, 1), 0)
-    member, device = place // (N * N), place % (N * N)
-    perm[...] = one_hot(
-        device // N + N * (2 * (device % N) + member) == momentum_map[...]
-    )
-    part, early, late = (place // CELLS) % 4, (place // TILE) % TILE, place % TILE
-    lane = (late // 2) * LANES + ((member * 4 + part) * 2 + late % 2) * TILE + early
-    select[...] = one_hot(lane == lax.broadcasted_iota(jnp.int32, (1, K), 1))
     def passed_on(step, carry):
         other = lax.rem(row + step, N)
 
@@ -371,7 +373,7 @@
     lax.fori_loop(0, N, passed_on, 0)
     rows_left(site_out, site_in, SITE)
     rows_left(ga_out, ga_in, GREEN_A)
-    cols_left(gb_out, gb_in, GREEN_B, to_window)
+    cols_left(gb_out, gb_in, GREEN_B, plain)
     rows_left(y_out, y_in, INNER)
     cols_left(s_out, s_in, SIGMA, plain)
 
@@ -444,7 +446,6 @@
     by_row = pltpu.VMEM((N, 2, BLOCK, LANES), BF16)
     by_col = pltpu.VMEM((N, 2, 4, TILE, LANES), BF16)
     wide = pltpu.VMEM((N, TILE, WIDE), BF16)
-    window = pltpu.VMEM((2, 4, N, TILE, LANES), BF16)
     halves = pltpu.VMEM((2, 2 * BLOCK, WIDE), BF16)
     return pl.pallas_call(
         kernel,
@@ -463,7 +464,7 @@
             pltpu.VMEM((LANES, WIDE), BF16),
             by_row, by_row, by_row,
             wide, wide, wide, wide,
-            by_row, by_row, by_col, window,
+            by_row, by_row, by_col, by_col,
             pltpu.VMEM((2, 2, 2 * LANES, 4 * LANES), BF16),
             pltpu.VMEM((2 * K, LANES), F32),
             pltpu.VMEM((K, K), BF16),

time: 55.6 us -> 55.8 us (level)
  no operation moved by 1% of the time
where the time goes in v7:
time: 55.8 us; the launch traced here: 55.7 us
  Pallas kernels  53.1 us (95%)
  local copies, waits for them, and re-layouts  1.31 us (2%)
  between operations  1.29 us (2%)
    pallas_call x1, Pallas kernels, body(): pl.pallas_call(kernel, out_shape=(tile, tile), in_specs=[pl.BlockSpec(mem...  53.1 us
    unnamed x2, local copies, waits for them, and re-layouts  1.31 us

profile of v7, /device:TPU:1, one launch (start us, length us, event | category | flops | bytes accessed | tf_op | source)
XLA Modules:
  0.0 55.7 jit_solution(14470550966448225611)
XLA Ops:
  1.3 53.1 %shard_map.86 = (bf16[2,8,8,512]{3,2,1,0:T(8,128)(2,1)S(1)}, bf16[2,8,8,512]{3,2,1,0:T(8,128)(2,1)S(1)}) custom-call(s32[1]{0:T(128)S(6)} %copy.11.offset_ref, s32[1,512]{1,0:T(1,128)} %bitcast.1, bf16[2,8,8,512]{3,2,1,0:T(8,128)(2,1)} %lesser_hbm.1, bf16[2,8,8,512]{3,2,1,0:T(8,128)(2,1)} %greater_hbm.1, bf16[512,1024]{1,0:T(8,128)(2,1)} %constant.6.clone.table_hbm, ...), custom_call_target="tpu_custom_call" | custom-call | tf_op jit(solution)/shard_map/pallas_call | solution.py:450
  54.4 0.7 %copy.12 = bf16[2,8,8,512]{3,2,1,0:T(8,128)(2,1)} copy(bf16[2,8,8,512]{3,2,1,0:T(8,128)(2,1)S(1)} %get-tuple-element.4) | data formatting | bytes 262144
  55.0 0.7 %copy.13 = bf16[2,8,8,512]{3,2,1,0:T(8,128)(2,1)} copy(bf16[2,8,8,512]{3,2,1,0:T(8,128)(2,1)S(1)} %get-tuple-element.5) | data formatting | bytes 262144
